TPU v7x, 32 devices: a whole 2x2x4 slice. The times are simulated.
32 devices in a mesh: expert: 16 (over z, y, x), dp: 2 (over core).
Axes of the slice: x: 2, y: 2, z: 4, core: 2. Of those that a mesh axis runs over, the one named last changes fastest.
Arguments:
- tokens: bfloat16 [4096, 2048], P(('expert', 'dp')), may hold values from -6 to 6
- routes: int32 [4096, 8], P(('expert', 'dp')), may hold values from 0 to 15, all different within a row; in each aligned block of 128 rows (0 to 127, 128 to 255, ...) at most 72 rows name the same one
- gates: float32 [4096, 8], P(('expert', 'dp')), may hold values from 0.05 to 1
- cotangent: bfloat16 [4096, 2048], P(('expert', 'dp')), may hold values from -6 to 6
- owner_before: int32 [16], replicated, may hold values from 0 to 15, each once
- owner_after: int32 [16], replicated, may hold values from 0 to 15, each once
- weights: bfloat16 [2, 16, 2048, 768], P(None, 'expert', 'dp'), may hold values from -6 to 6
- m_codes: bfloat16 [2, 16, 2048, 768], P(None, 'expert', 'dp'), may hold values from -7 to 7, as said below
- v_codes: bfloat16 [2, 16, 2048, 768], P(None, 'expert', 'dp'), may hold values from 1 to 7, as said below
- m_scales: bfloat16 [2, 16, 2048], P(None, 'expert', 'dp'), may hold values from 0.049804688 to 0.5
- v_scales: bfloat16 [2, 16, 2048], P(None, 'expert', 'dp'), may hold values from 0.019897461 to 0.19921875
- noise: bfloat16 [2, 16, 2048, 768], P(None, 'expert', 'dp'), may hold values from 0 to 1
Outputs:
- new_weights: bfloat16 [2, 16, 2048, 768], P(None, 'expert', 'dp')
- new_m_codes: bfloat16 [2, 16, 2048, 768], P(None, 'expert', 'dp')
- new_v_codes: bfloat16 [2, 16, 2048, 768], P(None, 'expert', 'dp')
- new_m_scales: bfloat16 [2, 16, 2048], P(None, 'expert', 'dp')
- new_v_scales: bfloat16 [2, 16, 2048], P(None, 'expert', 'dp')
Inputs may be any that keep to these rules, and one draw needn't show every extreme that they name: `routes`: in the rows of one device no expert is chosen by more than 72 tokens; each token chooses 8 different experts. `owner_before`: A permutation of the slots. `owner_after`: A permutation of the slots. `m_codes`: whole numbers. `v_codes`: whole numbers.
All inputs are finite; a program needn't handle non-finite values. Where the computation divides by a largest or mean magnitude, that divisor is 1e-20 or more.
Results may differ from a plain program's by a relative error of at most 0.022.
Values may be sent and summed in bfloat16 or wider, within the bound.
A program may use at most 128 MiB of HBM per device.

v0:
```python
import jax
import jax.numpy as jnp
from jax import lax
from jax.sharding import PartitionSpec as P

LEVELS = 7


learn_rate = 0.1
beta_one = 0.9
beta_two = 0.95
adam_step = 20.0
adam_epsilon = 1e-08
scale_epsilon = 1e-06


def transposed_dot(left, right):
    return lax.dot_general(
        left, right, (((0,), (0,)), ((), ())), preferred_element_type=jnp.float32
    )


def on_device(
    tokens,
    routes,
    gates,
    cotangent,
    owner_before,
    owner_after,
    weights,
    m_codes,
    v_codes,
    m_scales,
    v_scales,
    noise,
):
    expert_count = lax.axis_size("expert")
    slot_ids = jnp.arange(expert_count, dtype=jnp.int32)
    matches = (owner_after[None, :] == slot_ids[:, None]).astype(jnp.int32)
    source_slot = jnp.sum(matches * owner_before[None, :], axis=1)
    rows_dp = weights.shape[2]
    hidden_units = weights.shape[3]
    model_width = tokens.shape[1]
    piece_width = hidden_units // expert_count
    scale_pack = jnp.concatenate([m_scales.reshape(2 * rows_dp), v_scales.reshape(2 * rows_dp)])
    scale_copies = jnp.broadcast_to(scale_pack[:, None], (4 * rows_dp, expert_count))
    outgoing = (
        weights.reshape(2 * rows_dp, hidden_units),
        m_codes.reshape(2 * rows_dp, hidden_units),
        v_codes.reshape(2 * rows_dp, hidden_units),
        scale_copies,
    )
    spread = (
        lax.all_to_all(outgoing[0], "expert", split_axis=1, concat_axis=1, tiled=True),
        lax.all_to_all(outgoing[1], "expert", split_axis=1, concat_axis=1, tiled=True),
        lax.all_to_all(outgoing[2], "expert", split_axis=1, concat_axis=1, tiled=True),
        lax.all_to_all(outgoing[3], "expert", split_axis=1, concat_axis=1, tiled=True),
    )

    def regroup(array, block_width):
        shaped = array.reshape(array.shape[0], expert_count, block_width)
        return jnp.take(shaped, source_slot, axis=1).reshape(
            array.shape[0], expert_count * block_width
        )

    regrouped = (
        regroup(spread[0], piece_width),
        regroup(spread[1], piece_width),
        regroup(spread[2], piece_width),
        regroup(spread[3], 1),
    )
    arrived = (
        lax.all_to_all(regrouped[0], "expert", split_axis=1, concat_axis=1, tiled=True),
        lax.all_to_all(regrouped[1], "expert", split_axis=1, concat_axis=1, tiled=True),
        lax.all_to_all(regrouped[2], "expert", split_axis=1, concat_axis=1, tiled=True),
        lax.all_to_all(regrouped[3], "expert", split_axis=1, concat_axis=1, tiled=True),
    )
    moved_weights = arrived[0].reshape(2, rows_dp, hidden_units)
    moved_m = arrived[1].reshape(2, rows_dp, hidden_units)
    moved_v = arrived[2].reshape(2, rows_dp, hidden_units)
    moved_scales = arrived[3][:, 0]
    old_m_scales = moved_scales[: 2 * rows_dp].reshape(2, rows_dp)
    old_v_scales = moved_scales[2 * rows_dp :].reshape(2, rows_dp)
    token_count = tokens.shape[0]
    top_count = routes.shape[1]
    capacity = token_count * top_count * 9 // (8 * expert_count)
    entries = routes.reshape(-1)
    onehot = (entries[:, None] == slot_ids[None, :]).astype(jnp.int32)
    ranks = jnp.sum((jnp.cumsum(onehot, axis=0) - 1) * onehot, axis=1)
    targets = jnp.sum(onehot * owner_after[None, :], axis=1)
    positions = targets * capacity + ranks
    table = (
        jnp.full((expert_count * capacity,), -1, jnp.int32)
        .at[positions]
        .set(jnp.arange(entries.shape[0], dtype=jnp.int32))
    )
    live = table >= 0
    safe = jnp.where(live, table, 0)
    token_rows = safe // top_count
    token_block = jnp.where(live[:, None], tokens[token_rows], jnp.zeros((), jnp.bfloat16))
    gate_rows = jnp.where(live, gates.reshape(-1)[safe], 0.0)
    gated_block = (gate_rows[:, None] * cotangent[token_rows].astype(jnp.float32)).astype(
        jnp.bfloat16
    )
    arrived_tokens, arrived_grads = (
        lax.all_to_all(token_block, "expert", split_axis=0, concat_axis=0, tiled=True),
        lax.all_to_all(gated_block, "expert", split_axis=0, concat_axis=0, tiled=True),
    )
    scale_model = model_width ** (-0.5)
    scale_hidden = hidden_units ** (-0.5)
    full_weights = lax.all_gather(moved_weights, "dp", axis=1, tiled=True)
    pre_sum = jnp.dot(arrived_tokens, full_weights[0], preferred_element_type=jnp.float32)
    back_sum = jnp.dot(arrived_grads, full_weights[1], preferred_element_type=jnp.float32)
    pre = pre_sum * scale_model
    hidden = jax.nn.silu(pre).astype(jnp.bfloat16)
    back = back_sum * scale_hidden
    sigmoid_pre = jax.nn.sigmoid(pre)
    pre_grad = (back * sigmoid_pre * (1.0 + pre * (1.0 - sigmoid_pre))).astype(jnp.bfloat16)
    up_part = transposed_dot(arrived_tokens, pre_grad) * scale_model
    down_part = transposed_dot(arrived_grads, hidden) * scale_hidden
    summed = lax.psum_scatter(
        jnp.concatenate([up_part, down_part], axis=1).astype(jnp.bfloat16),
        "dp",
        scatter_dimension=0,
        tiled=True,
    ).astype(jnp.float32)
    grads = jnp.stack([summed[:, :hidden_units], summed[:, hidden_units:]])
    m_old = moved_m.astype(jnp.float32) * old_m_scales.astype(jnp.float32)[:, :, None] / LEVELS
    v_old = moved_v.astype(jnp.float32) * old_v_scales.astype(jnp.float32)[:, :, None] / LEVELS
    m_new = beta_one * m_old + (1.0 - beta_one) * grads
    v_new = beta_two * v_old + (1.0 - beta_two) * grads * grads
    direction = (
        m_new
        / (1.0 - beta_one**adam_step)
        / (jnp.sqrt(v_new / (1.0 - beta_two**adam_step)) + adam_epsilon)
    )
    new_weights = (moved_weights.astype(jnp.float32) - learn_rate * direction).astype(jnp.bfloat16)
    new_m_scales = lax.optimization_barrier(
        (jnp.max(jnp.abs(m_new), axis=2) + scale_epsilon).astype(jnp.bfloat16)
    )
    new_v_scales = lax.optimization_barrier(
        (jnp.max(v_new, axis=2) + scale_epsilon).astype(jnp.bfloat16)
    )
    dither = noise[:, 0].astype(jnp.float32)
    m_value = LEVELS * m_new / new_m_scales.astype(jnp.float32)[:, :, None] + (dither - 0.5)
    v_value = LEVELS * v_new / new_v_scales.astype(jnp.float32)[:, :, None] + dither
    new_m_codes = jnp.clip(m_value, -1.0 * LEVELS, 1.0 * LEVELS).astype(jnp.bfloat16)
    new_v_codes = jnp.clip(v_value, 0.0, 1.0 * LEVELS).astype(jnp.bfloat16)
    return (
        new_weights.reshape(2, 1, rows_dp, hidden_units),
        new_m_codes.reshape(2, 1, rows_dp, hidden_units),
        new_v_codes.reshape(2, 1, rows_dp, hidden_units),
        new_m_scales.reshape(2, 1, rows_dp),
        new_v_scales.reshape(2, 1, rows_dp),
    )


def solution(mesh):
    placed = (
        P(("expert", "dp"), None),
        P(("expert", "dp"), None),
        P(("expert", "dp"), None),
        P(("expert", "dp"), None),
        P(),
        P(),
        P(None, "expert", "dp", None),
        P(None, "expert", "dp", None),
        P(None, "expert", "dp", None),
        P(None, "expert", "dp"),
        P(None, "expert", "dp"),
        P(None, "expert", "dp", None),
    )
    return jax.shard_map(
        on_device,
        mesh=mesh,
        in_specs=placed,
        out_specs=(
            P(None, "expert", "dp", None),
            P(None, "expert", "dp", None),
            P(None, "expert", "dp", None),
            P(None, "expert", "dp"),
            P(None, "expert", "dp"),
        ),
        check_vma=False,
    )
```

profile of v0, /device:TPU:12, one launch (start us, length us, event | category | flops | bytes accessed | tf_op | source)
XLA Modules:
  0.0 846.2 jit_solution(6171264451363118570)
XLA Ops:
  7.2 8.8 %copy.95 = bf16[2,1,1024,768]{2,0,3,1:T(2,128)(2,1)} copy(bf16[2,1,1024,768]{3,2,1,0:T(8,128)(2,1)} %param.20) | data formatting | bytes 6291456 | tf_op args[6]
  16.0 6.1 all_to_all.52
  22.1 7.2 all-to-all-start
  29.3 8.7 %copy.96 = bf16[2,1,1024,768]{2,0,3,1:T(2,128)(2,1)} copy(bf16[2,1,1024,768]{3,2,1,0:T(8,128)(2,1)} %param.21) | data formatting | bytes 6291456 | tf_op args[7]
  38.0 6.1 all_to_all.55
  44.1 55.8 %all-to-all-done = bf16[2048,16,48]{0,2,1:T(8,128)(2,1)} async-done(((bf16[2048,16,48]{0,2,1:T(8,128)(2,1)}), bf16[2048,16,48]{0,2,1:T(8,128)(2,1)}, u32[]{:S(2)}, u32[]{:S(2)}) %all-to-all-start) | async-done | bytes 3145760 | tf_op jit(solution)/shard_map/all_to_all | solution.py:54
  105.4 8.7 %copy.106 = bf16[2,1,1024,768]{2,0,3,1:T(2,128)(2,1)} copy(bf16[2,1,1024,768]{3,2,1,0:T(8,128)(2,1)} %param.22) | data formatting | bytes 6291456 | tf_op args[8]
  120.2 55.1 %all-to-all-done.2 = bf16[2048,16,48]{0,2,1:T(8,128)(2,1)} async-done(((bf16[2048,16,48]{0,2,1:T(8,128)(2,1)}), bf16[2048,16,48]{0,2,1:T(8,128)(2,1)}, u32[]{:S(2)}, u32[]{:S(2)}) %all-to-all-start.2) | async-done | bytes 3145760 | tf_op jit(solution)/shard_map/all_to_all | solution.py:55
  191.8 58.4 %all-to-all-done.8 = bf16[2048,16,48]{0,2,1:T(8,128)(2,1)} async-done(((bf16[2048,16,48]{0,2,1:T(8,128)(2,1)}), bf16[2048,16,48]{0,2,1:T(8,128)(2,1)}, u32[]{:S(2)}, u32[]{:S(2)}) %all-to-all-start.8) | async-done | bytes 3145760 | tf_op jit(solution)/shard_map/all_to_all | solution.py:56
  259.3 6.5 select_bitcast_fusion
  265.8 6.9 all-to-all-start.1
  293.4 48.9 %all-to-all-done.1 = bf16[2048,16,48]{0,2,1:T(8,128)(2,1)} async-done(((bf16[2048,16,48]{0,2,1:T(8,128)(2,1)}), bf16[2048,16,48]{0,2,1:T(8,128)(2,1)}, u32[]{:S(2)}, u32[]{:S(2)}) %all-to-all-start.1) | async-done | bytes 3145760 | tf_op jit(solution)/shard_map/all_to_all | solution.py:73
  358.0 6.1 reshape.481
  369.4 81.9 %all-to-all-done.6 = bf16[16,72,2048]{2,1,0:T(8,128)(2,1)} async-done(((bf16[16,72,2048]{2,1,0:T(8,128)(2,1)}), bf16[16,72,2048]{2,1,0:T(8,128)(2,1)}, u32[]{:S(2)}, u32[]{:S(2)}) %all-to-all-start.6) | async-done | bytes 4718624 | tf_op jit(solution)/shard_map/all_to_all | solution.py:106
  457.6 13.6 %fusion.34 = (bf16[1,2048,768]{1,0,2:T(2,128)(2,1)}, bf16[1,2048,768]{1,0,2:T(2,128)(2,1)}) fusion(bf16[2,2048,768]{1,0,2:T(2,128)(2,1)} %all-gather.2.cloned.1.call-done), kind=kLoop, calls=%fused_computation.101 | loop fusion | bytes 12582912 | tf_op jit(solution)/shard_map/slice | solution.py:113
  471.1 15.1 %copy.105 = bf16[1,2048,768]{2,1,0:T(8,128)(2,1)} copy(bf16[1,2048,768]{1,0,2:T(2,128)(2,1)} %get-tuple-element.52) | data formatting | bytes 6291456 | tf_op jit(solution)/shard_map/slice | solution.py:112
  486.2 15.7 %copy.104 = bf16[1,2048,768]{2,1,0:T(8,128)(2,1)} copy(bf16[1,2048,768]{1,0,2:T(2,128)(2,1)} %get-tuple-element.51) | data formatting | bytes 6291456 | tf_op jit(solution)/shard_map/slice | solution.py:113
  501.9 9.0 %convolution_multiply_fusion = f32[1152,768]{1,0:T(8,128)} fusion(bf16[1152,2048]{1,0:T(8,128)(2,1)} %bitcast.11, bf16[1,2048,768]{2,1,0:T(8,128)(2,1)} %copy.105), kind=kOutput, calls=%fused_computation.36 | convolution fusion | flops 3624763392 | bytes 11403264 | tf_op jit(solution)/shard_map/dot_general | solution.py:112
  510.9 49.7 %all-to-all-done.7 = bf16[16,72,2048]{2,1,0:T(8,128)(2,1)} async-done(((bf16[16,72,2048]{2,1,0:T(8,128)(2,1)}), bf16[16,72,2048]{2,1,0:T(8,128)(2,1)}, u32[]{:S(2)}, u32[]{:S(2)}) %all-to-all-start.7) | async-done | bytes 4718624 | tf_op jit(solution)/shard_map/all_to_all | solution.py:107
  560.6 9.4 %multiply_convert_fusion = bf16[2048,768]{0,1:T(8,128)(2,1)} fusion(bf16[1152,2048]{1,0:T(8,128)(2,1)} %bitcast.13, f32[1152,768]{1,0:T(8,128)} %convolution_multiply_fusion), kind=kOutput, calls=%fused_computation.33 | convolution fusion | flops 3631448064 | bytes 11403264 | tf_op jit(solution)/shard_map/dot_general | solution.py:18
  570.1 22.8 %multiply_convert_fusion.1 = bf16[2048,768]{0,1:T(8,128)(2,1)} fusion(bf16[1152,2048]{1,0:T(8,128)(2,1)} %bitcast.11, f32[1152,768]{1,0:T(8,128)} %convolution_multiply_fusion, bf16[1152,2048]{1,0:T(8,128)(2,1)} %bitcast.13, bf16[1,2048,768]{2,1,0:T(8,128)(2,1)} %copy.104), kind=kOutput, calls=%fused_computation.34 | convolution fusion | flops 7259750400 | bytes 19267584 | tf_op jit(solution)/shard_map/dot_general | solution.py:18
  592.9 6.6 pad_maximum_fusion
  601.3 11.0 %all_to_all.78 = bf16[16,2,2048]{2,1,0:T(2,128)(2,1)S(1)} all-to-all(bf16[16,2,2048]{2,1,0:T(2,128)(2,1)S(1)} %reshape.586), channel_id=1, replica_groups=mesh['expert'=16,'dp'=2] {'expert'}, dimensions={0} | all-to-all | bytes 262144 | tf_op jit(solution)/shard_map/all_to_all | solution.py:76
  612.4 74.8 %all_to_all.79 = bf16[2048,16,48]{0,2,1:T(8,128)(2,1)} all-to-all(bf16[2048,16,48]{0,2,1:T(8,128)(2,1)} %get-tuple-element.56), channel_id=1, replica_groups=mesh['expert'=16,'dp'=2] {'expert'}, dimensions={1} | all-to-all | bytes 6291456 | tf_op jit(solution)/shard_map/all_to_all | solution.py:74
  698.1 9.1 %reshape.484 = f32[2,1,1024,768]{2,0,3,1:T(2,128)} reshape(bf16[2048,16,48]{0,2,1:T(8,128)(2,1)} %all-to-all-done.1) | data formatting | bytes 9437184 | tf_op jit(solution)/shard_map/convert_element_type | solution.py:137
  707.2 9.1 %reshape.485 = f32[2,1,1024,768]{2,0,3,1:T(2,128)} reshape(bf16[2048,16,48]{0,2,1:T(8,128)(2,1)} %all_to_all.79) | data formatting | bytes 9437184 | tf_op jit(solution)/shard_map/convert_element_type | solution.py:128
  716.2 45.5 %all-to-all-done.9 = bf16[2048,16,48]{0,2,1:T(8,128)(2,1)} async-done(((bf16[2048,16,48]{0,2,1:T(8,128)(2,1)}), bf16[2048,16,48]{0,2,1:T(8,128)(2,1)}, u32[]{:S(2)}, u32[]{:S(2)}) %all-to-all-start.9) | async-done | bytes 3145760 | tf_op jit(solution)/shard_map/all_to_all | solution.py:75
  761.8 9.1 %reshape.488 = f32[2,1,1024,768]{2,0,3,1:T(2,128)} reshape(bf16[2048,16,48]{0,2,1:T(8,128)(2,1)} %all-to-all-done.9) | data formatting | bytes 9437184 | tf_op jit(solution)/shard_map/convert_element_type | solution.py:129
  780.7 10.2 %copy.109 = f32[2,1024,768]{1,0,2:T(2,128)} copy(f32[2,1024,768]{1,2,0:T(8,128)} %pad_maximum_fusion.2) | data formatting | bytes 12582912 | tf_op jit(solution)/shard_map/stack | solution.py:127
  791.0 9.2 %stack.23 = f32[2048,16,48]{0,2,1:T(8,128)} reshape(f32[2,1024,768]{1,0,2:T(2,128)} %copy.109) | data formatting | bytes 12582912 | tf_op jit(solution)/shard_map/stack | solution.py:127
  800.2 6.2 fusion.8
  806.4 18.5 %fusion.5 = (bf16[2,1,1024,768]{2,3,1,0:T(8,128)(2,1)}, bf16[2,1,1024,768]{2,3,1,0:T(8,128)(2,1)}, bf16[2,1,1024,768]{2,3,1,0:T(8,128)(2,1)}) fusion(bf16[2,1,1024,768]{2,3,1,0:T(8,128)(2,1)} %copy.110, f32[2,1024]{1,0:T(2,128)S(1)} %convert_element_type.186, f32[1,1,1024,768]{2,3,1,0:T(8,128)} %get-tuple-element.49, ...), kind=kLoop, calls=%fused_computation.18 | loop fusion | flops 45613056 | bytes 37781504 | tf_op jit(solution)/shard_map/convert_element_type | solution.py:148
  (107 shorter events, 121.3 us)
Async XLA Ops:
  7.2 275.4 %copy-start = (bf16[128,2048]{1,0:T(8,128)(2,1)S(1)}, bf16[128,2048]{1,0:T(8,128)(2,1)}, u32[]{:S(2)}) copy-start(bf16[128,2048]{1,0:T(8,128)(2,1)} %param.14) | copy-start | bytes 1572868
  22.1 77.8 %all-to-all-start = ((bf16[2048,16,48]{0,2,1:T(8,128)(2,1)}), bf16[2048,16,48]{0,2,1:T(8,128)(2,1)}, u32[]{:S(2)}, u32[]{:S(2)}) async-start(bf16[2048,16,48]{0,2,1:T(8,128)(2,1)} %all_to_all.52), calls=%async_computation | async-start | bytes 6291456 | tf_op jit(solution)/shard_map/all_to_all | solution.py:54
  99.9 75.5 %all-to-all-start.2 = ((bf16[2048,16,48]{0,2,1:T(8,128)(2,1)}), bf16[2048,16,48]{0,2,1:T(8,128)(2,1)}, u32[]{:S(2)}, u32[]{:S(2)}) async-start(bf16[2048,16,48]{0,2,1:T(8,128)(2,1)} %all_to_all.55), calls=%async_computation.2 | async-start | bytes 6291456 | tf_op jit(solution)/shard_map/all_to_all | solution.py:55
  120.2 60.0 %copy-start.7 = (bf16[2,1,1024]{2,0,1:T(2,128)(2,1)S(1)}, bf16[2,1,1024]{2,0,1:T(2,128)(2,1)}, u32[]{:S(2)}) copy-start(bf16[2,1,1024]{2,0,1:T(2,128)(2,1)} %param.24) | copy-start | bytes 12292
  120.2 60.0 %copy-start.8 = (bf16[2,1,1024]{2,0,1:T(2,128)(2,1)S(1)}, bf16[2,1,1024]{2,0,1:T(2,128)(2,1)}, u32[]{:S(2)}) copy-start(bf16[2,1,1024]{2,0,1:T(2,128)(2,1)} %param.23) | copy-start | bytes 12292
  120.2 62.8 %copy-start.9 = (s32[16]{0:T(128)S(1)}, s32[16]{0:T(128)}, u32[]{:S(2)}) copy-start(s32[16]{0:T(128)} %param.19) | copy-start | bytes 196
  120.2 62.8 %copy-start.10 = (s32[16]{0:T(128)S(1)}, s32[16]{0:T(128)}, u32[]{:S(2)}) copy-start(s32[16]{0:T(128)} %param.18) | copy-start | bytes 196
  175.4 74.8 %all-to-all-start.8 = ((bf16[2048,16,48]{0,2,1:T(8,128)(2,1)}), bf16[2048,16,48]{0,2,1:T(8,128)(2,1)}, u32[]{:S(2)}, u32[]{:S(2)}) async-start(bf16[2048,16,48]{0,2,1:T(8,128)(2,1)} %all_to_all.65), calls=%async_computation.9 | async-start | bytes 6291456 | tf_op jit(solution)/shard_map/all_to_all | solution.py:56
  250.2 15.6 %all-to-all-start.4 = ((bf16[16,2,2048]{2,1,0:T(2,128)(2,1)}), bf16[16,2,2048]{2,1,0:T(2,128)(2,1)S(1)}, u32[]{:S(2)}, u32[]{:S(2)}) async-start(bf16[16,2,2048]{2,1,0:T(2,128)(2,1)} %reshape.584), calls=%async_computation.4 | async-start | bytes 262144 | tf_op jit(solution)/shard_map/all_to_all | solution.py:57
  265.8 6.9 copy-start.5
  265.8 76.4 %all-to-all-start.1 = ((bf16[2048,16,48]{0,2,1:T(8,128)(2,1)}), bf16[2048,16,48]{0,2,1:T(8,128)(2,1)}, u32[]{:S(2)}, u32[]{:S(2)}) async-start(bf16[2048,16,48]{0,2,1:T(8,128)(2,1)} %get-tuple-element.57), calls=%async_computation.1 | async-start | bytes 6291456 | tf_op jit(solution)/shard_map/all_to_all | solution.py:73
  293.4 53.7 %copy-start.2 = (bf16[128,2048]{1,0:T(8,128)(2,1)S(1)}, bf16[128,2048]{1,0:T(8,128)(2,1)}, u32[]{:S(2)}) copy-start(bf16[128,2048]{1,0:T(8,128)(2,1)} %param.17) | copy-start | bytes 1572868
  342.3 109.0 %all-to-all-start.6 = ((bf16[16,72,2048]{2,1,0:T(8,128)(2,1)}), bf16[16,72,2048]{2,1,0:T(8,128)(2,1)}, u32[]{:S(2)}, u32[]{:S(2)}) async-start(bf16[16,72,2048]{2,1,0:T(8,128)(2,1)} %broadcast_select_fusion), calls=%async_computation.6 | async-start | bytes 9437184 | tf_op jit(solution)/shard_map/all_to_all | solution.py:106
  347.1 6.0 copy-start.6
  347.1 110.5 %all-gather.2.cloned.1.call-start = ((), (), s32[]{:S(2)}) async-start(), calls=%async_computation.11 | async-start | bytes 9437184 | tf_op jit(solution)/shard_map/all_gather | solution.py:111
  451.3 109.4 %all-to-all-start.7 = ((bf16[16,72,2048]{2,1,0:T(8,128)(2,1)}), bf16[16,72,2048]{2,1,0:T(8,128)(2,1)}, u32[]{:S(2)}, u32[]{:S(2)}) async-start(bf16[16,72,2048]{2,1,0:T(8,128)(2,1)} %fusion), calls=%async_computation.7 | async-start | bytes 9437184 | tf_op jit(solution)/shard_map/all_to_all | solution.py:107
  456.5 314.3 %reduce-scatter.2.cloned.1.call-start = ((), (), s32[]{:S(2)}) async-start(), calls=%async_computation.12 | async-start | bytes 9437184 | tf_op jit(solution)/shard_map/reduce_scatter | solution.py:121
  687.1 74.6 %all-to-all-start.9 = ((bf16[2048,16,48]{0,2,1:T(8,128)(2,1)}), bf16[2048,16,48]{0,2,1:T(8,128)(2,1)}, u32[]{:S(2)}, u32[]{:S(2)}) async-start(bf16[2048,16,48]{0,2,1:T(8,128)(2,1)} %get-tuple-element.55), calls=%async_computation.10 | async-start | bytes 6291456 | tf_op jit(solution)/shard_map/all_to_all | solution.py:75
  806.4 18.5 %copy-start.3 = (bf16[2,1024]{1,0:T(2,128)(2,1)}, bf16[2,1024]{1,0:T(2,128)(2,1)S(1)}, u32[]{:S(2)}) copy-start(bf16[2,1024]{1,0:T(2,128)(2,1)S(1)} %convert_element_type.177) | copy-start | bytes 12292
  806.4 18.5 %copy-start.4 = (bf16[2,1024]{1,0:T(2,128)(2,1)}, bf16[2,1024]{1,0:T(2,128)(2,1)S(1)}, u32[]{:S(2)}) copy-start(bf16[2,1024]{1,0:T(2,128)(2,1)S(1)} %convert_element_type.185) | copy-start | bytes 12292
  829.5 9.3 %copy-start.1 = (bf16[128,2048]{1,0:T(8,128)(2,1)S(1)}, bf16[128,2048]{1,0:T(8,128)(2,1)}, u32[]{:S(2)}) copy-start(bf16[128,2048]{1,0:T(8,128)(2,1)} %param.14) | copy-start | bytes 1572868
Sparse Core Ops, SparseCore 0:
  364.2 16.5 all-gather.1
  599.6 13.5 reduce-scatter.1
where the time goes:
time: 859 us; the launch traced here: 846 us
  waiting for transfers between devices  395 us (46%)
  local copies, waits for them, and re-layouts  202 us (24%)
  blocking collectives  85.8 us (10%)
  other arithmetic  61.5 us (7%)
  starting transfers between devices  45.2 us (5%)
  matrix products  41.2 us (5%)
  between operations  14.9 us (2%)
    all_to_all x1, waiting for transfers between devices, on_device(): lax.all_to_all(token_block, 'expert', split_axis=0, concat_axis=0, tiled=...  81.9 us
    all_to_all x1, blocking collectives, on_device(): lax.all_to_all(regrouped[1], 'expert', split_axis=1, concat_axis=1, tiled...  74.8 us
    all_to_all x1, waiting for transfers between devices, on_device(): lax.all_to_all(outgoing[2], 'expert', split_axis=1, concat_axis=1, tiled=...  58.4 us
    all_to_all x1, waiting for transfers between devices, on_device(): lax.all_to_all(outgoing[0], 'expert', split_axis=1, concat_axis=1, tiled=...  55.8 us
    all_to_all x1, waiting for transfers between devices, on_device(): lax.all_to_all(outgoing[1], 'expert', split_axis=1, concat_axis=1, tiled=...  55.1 us
    all_to_all x1, waiting for transfers between devices, on_device(): lax.all_to_all(gated_block, 'expert', split_axis=0, concat_axis=0, tiled=...  49.7 us
    all_to_all x1, waiting for transfers between devices, on_device(): lax.all_to_all(regrouped[0], 'expert', split_axis=1, concat_axis=1, tiled...  48.9 us
    unnamed x39, local copies, waits for them, and re-layouts  47.2 us
  transfers between devices with their start and end apart: 10, of which 7 were waited for; matrix products, arithmetic and copies ran while one was open for 20% of the time, Pallas kernels for 0%

commit v1 on v0

v1 whole, which is shorter than its diff:
```python
import functools

import jax
import jax.numpy as jnp
from jax import lax
from jax.experimental import pallas as pl
from jax.experimental.pallas import tpu as pltpu
from jax.sharding import PartitionSpec as P

LEVELS = 7


learn_rate = 0.1
beta_one = 0.9
beta_two = 0.95
adam_step = 20.0
adam_epsilon = 1e-08
scale_epsilon = 1e-06


def transposed_dot(left, right):
    return lax.dot_general(
        left, right, (((0,), (0,)), ((), ())), preferred_element_type=jnp.float32
    )


def adam_kernel(grad, weight, m_code, v_code, m_scale, v_scale, noise, new_w, new_m, new_v, new_ms, new_vs):
    grads = grad[...].astype(jnp.float32)
    m_old = m_code[...].astype(jnp.float32) * (m_scale[...].astype(jnp.float32) / LEVELS)
    v_old = v_code[...].astype(jnp.float32) * (v_scale[...].astype(jnp.float32) / LEVELS)
    m_new = beta_one * m_old + (1.0 - beta_one) * grads
    v_new = beta_two * v_old + (1.0 - beta_two) * grads * grads
    direction = (
        m_new
        * (1.0 / (1.0 - beta_one**adam_step))
        / (jnp.sqrt(v_new * (1.0 / (1.0 - beta_two**adam_step))) + adam_epsilon)
    )
    new_w[...] = (weight[...].astype(jnp.float32) - learn_rate * direction).astype(jnp.bfloat16)
    m_top = (jnp.max(jnp.abs(m_new), axis=1, keepdims=True) + scale_epsilon).astype(jnp.bfloat16)
    v_top = (jnp.max(v_new, axis=1, keepdims=True) + scale_epsilon).astype(jnp.bfloat16)
    new_ms[...] = m_top
    new_vs[...] = v_top
    dither = noise[...].astype(jnp.float32)
    m_value = m_new * (LEVELS / m_top.astype(jnp.float32)) + (dither - 0.5)
    v_value = v_new * (LEVELS / v_top.astype(jnp.float32)) + dither
    new_m[...] = jnp.clip(m_value, -1.0 * LEVELS, 1.0 * LEVELS).astype(jnp.bfloat16)
    new_v[...] = jnp.clip(v_value, 0.0, 1.0 * LEVELS).astype(jnp.bfloat16)


def adam(grads, weight, m_code, v_code, m_scale, v_scale, noise):
    rows, width = weight.shape
    block = min(256, rows)
    wide = pl.BlockSpec((block, width), lambda i: (i, 0))
    thin = pl.BlockSpec((block, 1), lambda i: (i, 0))
    big = jax.ShapeDtypeStruct((rows, width), jnp.bfloat16)
    small = jax.ShapeDtypeStruct((rows, 1), jnp.bfloat16)
    return pl.pallas_call(
        adam_kernel,
        grid=(rows // block,),
        out_shape=(big, big, big, small, small),
        in_specs=[wide, wide, wide, wide, thin, thin, wide],
        out_specs=(wide, wide, wide, thin, thin),
        name="adam",
        cost_estimate=pl.CostEstimate(
            flops=30 * rows * width, bytes_accessed=16 * rows * width, transcendentals=2 * rows * width
        ),
    )(grads, weight, m_code, v_code, m_scale, v_scale, noise)


def on_device(
    tokens,
    routes,
    gates,
    cotangent,
    owner_before,
    owner_after,
    weights,
    m_codes,
    v_codes,
    m_scales,
    v_scales,
    noise,
):
    expert_count = lax.axis_size("expert")
    me = lax.axis_index("expert")
    slot_ids = jnp.arange(expert_count, dtype=jnp.int32)
    matches = (owner_after[None, :] == slot_ids[:, None]).astype(jnp.int32)
    source_slot = jnp.sum(matches * owner_before[None, :], axis=1)
    my_match = (owner_after == me).astype(jnp.int32)
    my_expert = jnp.sum(my_match * slot_ids)
    my_source = jnp.sum(my_match * owner_before)
    rows_dp = weights.shape[2]
    hidden_units = weights.shape[3]
    model_width = tokens.shape[1]
    token_count = tokens.shape[0]
    piece = 2 * rows_dp // expert_count

    def spread(array):
        shaped = array.reshape(expert_count, piece, hidden_units)
        return lax.all_to_all(shaped, "expert", split_axis=0, concat_axis=0, tiled=True)

    def collect(array):
        regrouped = jnp.take(array, source_slot, axis=0)
        return lax.all_to_all(regrouped, "expert", split_axis=0, concat_axis=0, tiled=True)

    dense_gates = jnp.sum(
        jnp.where(routes[:, :, None] == slot_ids[None, None, :], gates[:, :, None], 0.0), axis=1
    ).T
    all_gates = lax.all_gather(dense_gates, "expert", axis=0, tiled=False)
    gate = lax.dynamic_index_in_dim(all_gates, my_expert, axis=1, keepdims=False).reshape(-1)
    all_tokens = lax.all_gather(tokens, "expert", axis=0, tiled=True)
    all_cotangent = lax.all_gather(cotangent, "expert", axis=0, tiled=True)
    scales = jnp.concatenate([m_scales.reshape(1, 2 * rows_dp), v_scales.reshape(1, 2 * rows_dp)])
    all_scales = lax.all_gather(scales, "expert", axis=0, tiled=False)
    old_scales = lax.dynamic_index_in_dim(all_scales, my_source, axis=0, keepdims=False)

    moved_weights = collect(spread(weights)).reshape(2, rows_dp, hidden_units)
    moved_m = collect(spread(m_codes)).reshape(2 * rows_dp, hidden_units)
    moved_v = collect(spread(v_codes)).reshape(2 * rows_dp, hidden_units)

    gated = (gate[:, None] * all_cotangent.astype(jnp.float32)).astype(jnp.bfloat16)
    scale_model = model_width ** (-0.5)
    scale_hidden = hidden_units ** (-0.5)
    full_weights = lax.all_gather(moved_weights, "dp", axis=1, tiled=True)
    pre = jnp.dot(all_tokens, full_weights[0], preferred_element_type=jnp.float32) * scale_model
    back = jnp.dot(gated, full_weights[1], preferred_element_type=jnp.float32) * scale_hidden
    sigmoid_pre = jax.nn.sigmoid(pre)
    hidden = (pre * sigmoid_pre).astype(jnp.bfloat16)
    pre_grad = (back * sigmoid_pre * (1.0 + pre * (1.0 - sigmoid_pre))).astype(jnp.bfloat16)
    up_part = transposed_dot(all_tokens, pre_grad) * scale_model
    down_part = transposed_dot(gated, hidden) * scale_hidden
    summed = lax.psum_scatter(
        jnp.stack([up_part.astype(jnp.bfloat16), down_part.astype(jnp.bfloat16)]),
        "dp",
        scatter_dimension=1,
        tiled=True,
    )
    new_w, new_m, new_v, new_ms, new_vs = adam(
        summed.reshape(2 * rows_dp, hidden_units),
        moved_weights.reshape(2 * rows_dp, hidden_units),
        moved_m,
        moved_v,
        old_scales[0][:, None],
        old_scales[1][:, None],
        noise.reshape(2 * rows_dp, hidden_units),
    )
    return (
        new_w.reshape(2, 1, rows_dp, hidden_units),
        new_m.reshape(2, 1, rows_dp, hidden_units),
        new_v.reshape(2, 1, rows_dp, hidden_units),
        new_ms.reshape(2, 1, rows_dp),
        new_vs.reshape(2, 1, rows_dp),
    )


def solution(mesh):
    placed = (
        P(("expert", "dp"), None),
        P(("expert", "dp"), None),
        P(("expert", "dp"), None),
        P(("expert", "dp"), None),
        P(),
        P(),
        P(None, "expert", "dp", None),
        P(None, "expert", "dp", None),
        P(None, "expert", "dp", None),
        P(None, "expert", "dp"),
        P(None, "expert", "dp"),
        P(None, "expert", "dp", None),
    )
    return jax.shard_map(
        on_device,
        mesh=mesh,
        in_specs=placed,
        out_specs=(
            P(None, "expert", "dp", None),
            P(None, "expert", "dp", None),
            P(None, "expert", "dp", None),
            P(None, "expert", "dp"),
            P(None, "expert", "dp"),
        ),
        check_vma=False,
    )
```

time: 859 us -> 782 us (0.910); the launches traced: 846 us -> 780 us
  blocking collectives: 85.8 us -> 348 us
  local copies, waits for them, and re-layouts: 202 us -> 16.1 us
  waiting for transfers between devices: 395 us -> 297 us
  other arithmetic: 61.5 us -> 12.2 us
  starting transfers between devices: 45.2 us -> 15.7 us
  matrix products: 41.2 us -> 58.5 us
  Pallas kernels: 0 us -> 14.3 us
    all_to_all x8 -> x3, waiting for transfers between devices: 395 us -> 210 us  [the longest x2 210 us: spread(): lax.all_to_all(shaped, 'expert', split_axis=0, concat_axis=0, tiled=True)]
    all_to_all x2 -> x3, blocking collectives: 85.8 us -> 228 us  [the longest x2 150 us: collect(): lax.all_to_all(regrouped, 'expert', split_axis=0, concat_axis=0, tiled=True)]
    all_gather x0 -> x2, blocking collectives: none -> 120 us  [the longest x1 90.4 us: on_device(): all_scales = lax.all_gather(scales, 'expert', axis=0, tiled=False)]
    all_gather x0 -> x2, waiting for transfers between devices: none -> 86.3 us  [the longest x1 86.3 us: on_device(): all_cotangent = lax.all_gather(cotangent, 'expert', axis=0, tiled=True)]
    unnamed x39 -> x18, local copies, waits for them, and re-layouts: 47.2 us -> 1.68 us
    slice x5 -> x0, local copies, waits for them, and re-layouts: 44.6 us -> none  [the longest x2 29.3 us: on_device(): full_weights[1]]
    all_to_all x8 -> x3, starting transfers between devices: 45.1 us -> 15.5 us  [the longest x2 10.4 us: spread(): lax.all_to_all(shaped, 'expert', split_axis=0, concat_axis=0, tiled=True)]
    convert_element_type x7 -> x0, local copies, waits for them, and re-layouts: 27.3 us -> none  [the longest x1 9.12 us: on_device(): moved_weights.astype(jnp.float32) - learn_rate * direction]
  transfers between devices with their start and end apart: 10 -> 7, of which waited for: 7 -> 3; matrix products, arithmetic and copies ran while one was open for 20% -> 4% of each run, Pallas kernels for 0% -> 0%
where the time goes in v1:
time: 782 us; the launch traced here: 780 us
  blocking collectives  348 us (45%)
  waiting for transfers between devices  297 us (38%)
  matrix products  58.5 us (7%)
  between operations  17.8 us (2%)
  local copies, waits for them, and re-layouts  16.1 us (2%)
  starting transfers between devices  15.7 us (2%)
  Pallas kernels  14.3 us (2%)
  other arithmetic  12.2 us (2%)
    all_to_all x2, waiting for transfers between devices, spread(): lax.all_to_all(shaped, 'expert', split_axis=0, concat_axis=0, tiled=True)  210 us
    all_to_all x2, blocking collectives, collect(): lax.all_to_all(regrouped, 'expert', split_axis=0, concat_axis=0, tiled=True)  150 us
    all_gather x1, blocking collectives, on_device(): all_scales = lax.all_gather(scales, 'expert', axis=0, tiled=False)  90.4 us
    all_gather x1, waiting for transfers between devices, on_device(): all_cotangent = lax.all_gather(cotangent, 'expert', axis=0, tiled=True)  86.3 us
    all_to_all x1, blocking collectives, spread(): lax.all_to_all(shaped, 'expert', split_axis=0, concat_axis=0, tiled=True)  77.4 us
    dot_general x2, matrix products, transposed_dot(): lax.dot_general(left, right, (((0,), (0,)), ((), ())), preferred_element_...  46.8 us
    all_gather x1, blocking collectives, on_device(): all_gates = lax.all_gather(dense_gates, 'expert', axis=0, tiled=False)  30 us
  transfers between devices with their start and end apart: 7, of which 3 were waited for; matrix products, arithmetic and copies ran while one was open for 4% of the time, Pallas kernels for 0%

profile of v1, /device:TPU:12, one launch (start us, length us, event | category | flops | bytes accessed | tf_op | source)
XLA Modules:
  0.0 779.8 jit_solution(10707597496686880661)
XLA Ops:
  7.2 77.4 %all_to_all.30 = bf16[16,128,768]{2,1,0:T(8,128)(2,1)} all-to-all(bf16[16,128,768]{2,1,0:T(8,128)(2,1)} %bitcast.87), channel_id=1, replica_groups=mesh['expert'=16,'dp'=2] {'expert'}, dimensions={0} | all-to-all | bytes 6291456 | tf_op jit(solution)/shard_map/all_to_all | solution.py:100
  84.5 5.2 all-to-all-start.2
  89.8 0.7 all-gather.11.cloned.1.call-update
  90.5 102.5 %all-to-all-done.2 = bf16[16,128,768]{2,1,0:T(8,128)(2,1)S(1)} async-done(((bf16[16,128,768]{2,1,0:T(8,128)(2,1)}), bf16[16,128,768]{2,1,0:T(8,128)(2,1)S(1)}, u32[]{:S(2)}, u32[]{:S(2)}) %all-to-all-start.2) | async-done | bytes 3145760 | tf_op jit(solution)/shard_map/all_to_all | solution.py:100
  193.0 5.2 all-to-all-start.4
  198.3 0.1 select_reduce_fusion.1
  198.4 4.3 gather_fusion
  202.7 2.4 gather_fusion.1
  205.1 107.1 %all-to-all-done.4 = bf16[16,128,768]{2,1,0:T(8,128)(2,1)} async-done(((bf16[16,128,768]{2,1,0:T(8,128)(2,1)}), bf16[16,128,768]{2,1,0:T(8,128)(2,1)}, u32[]{:S(2)}, u32[]{:S(2)}) %all-to-all-start.4) | async-done | bytes 3145760 | tf_op jit(solution)/shard_map/all_to_all | solution.py:100
  312.2 4.3 gather_fusion.2
  316.5 5.4 broadcast_select_fusion
  321.9 75.1 %all_to_all.31 = bf16[16,128,768]{2,1,0:T(8,128)(2,1)} all-to-all(bf16[16,128,768]{2,1,0:T(8,128)(2,1)S(1)} %get-tuple-element.42), channel_id=1, replica_groups=mesh['expert'=16,'dp'=2] {'expert'}, dimensions={0} | all-to-all | bytes 6291456 | tf_op jit(solution)/shard_map/all_to_all | solution.py:104
  397.0 0.0 all-gather.7.cloned.1.call-start
  397.1 0.7 all-gather.7.cloned.1.call-update
  397.8 0.6 fusion.20
  400.4 30.0 %all-gather = f32[256,128]{1,0:T(8,128)S(1)} all-gather(f32[16,128]{1,0:T(8,128)S(1)} %bitcast.93), channel_id=2, replica_groups=mesh['expert'=16,'dp'=2] {'expert'}, dimensions={0}, use_global_device_ids=true | all-gather | bytes 139264 | tf_op jit(solution)/shard_map/all_gather | solution.py:109
  430.4 11.7 %fusion.9 = f32[768,2048]{0,1:T(8,128)} fusion(bf16[2048,2048]{1,0:T(8,128)(2,1)} %all-gather.11.cloned.1.call-done, bf16[2,2048,768]{2,1,0:T(8,128)(2,1)} %all-gather.9.cloned.1.call-done), kind=kOutput, calls=%fused_computation.19 | convolution fusion | flops 6442450944 | bytes 17825792 | tf_op jit(solution)/shard_map/dot_general | solution.py:125
  442.1 86.3 %all-gather.7.cloned.1.call-done = bf16[2048,2048]{1,0:T(8,128)(2,1)} async-done(((bf16[128,2048]{1,0:T(8,128)(2,1)}), bf16[2048,2048]{1,0:T(8,128)(2,1)}) %all-gather.7.cloned.1.call-update) | async-done | bytes 8388624 | tf_op jit(solution)/shard_map/all_gather | solution.py:112
  528.4 34.8 %fusion.15 = bf16[1,2048,768]{2,1,0:T(8,128)(2,1)} fusion(bf16[2048,2048]{1,0:T(8,128)(2,1)} %all-gather.11.cloned.1.call-done, f32[768,2048]{0,1:T(8,128)} %fusion.9, bf16[2048,2048]{1,0:T(8,128)(2,1)} %all-gather.7.cloned.1.call-done, f32[2048]{0:T(1024)S(1)} %bitcast.94, bf16[2,2048,768]{2,1,0:T(8,128)(2,1)} %all-gather.9.cloned.1.call-done), kind=kOutput, calls=%fused_computation.29 | convolution fusion | flops 12917932032 | bytes 29368320 | tf_op jit(solution)/shard_map/dot_general | solution.py:22
  563.3 12.0 %fusion.16 = bf16[1,2048,768]{2,1,0:T(8,128)(2,1)S(1)} fusion(f32[768,2048]{0,1:T(8,128)} %fusion.9, bf16[2048,2048]{1,0:T(8,128)(2,1)} %all-gather.7.cloned.1.call-done, f32[2048]{0:T(1024)S(1)} %bitcast.95), kind=kOutput, calls=%fused_computation.30 | convolution fusion | flops 6467616768 | bytes 17833984 | tf_op jit(solution)/shard_map/dot_general | solution.py:22
  575.3 3.2 pad_maximum_fusion
  578.5 75.1 %all_to_all.32 = bf16[16,128,768]{2,1,0:T(8,128)(2,1)} all-to-all(bf16[16,128,768]{2,1,0:T(8,128)(2,1)S(1)} %get-tuple-element.41), channel_id=1, replica_groups=mesh['expert'=16,'dp'=2] {'expert'}, dimensions={0} | all-to-all | bytes 6291456 | tf_op jit(solution)/shard_map/all_to_all | solution.py:104
  653.7 5.1 all-to-all-start.5
  660.8 90.4 %all-gather.2 = bf16[16,2,2048]{2,1,0:T(2,128)(2,1)S(1)} all-gather(bf16[1,2,2048]{2,1,0:T(2,128)(2,1)S(1)} %maximum_bitcast_fusion), channel_id=3, replica_groups=mesh['expert'=16,'dp'=2] {'expert'}, dimensions={0}, use_global_device_ids=true | all-gather | bytes 139264 | tf_op jit(solution)/shard_map/all_gather | solution.py:114
  751.2 1.1 copy.44.m_scale
  752.3 1.1 copy.45.v_scale
  753.4 1.6 copy-done
  755.0 14.3 %adam.1 = (bf16[2048,768]{1,0:T(8,128)(2,1)}, bf16[2048,768]{1,0:T(8,128)(2,1)}, bf16[2048,768]{1,0:T(8,128)(2,1)}, bf16[2048,1]{1,0:T(8,128)(2,1)}, bf16[2048,1]{1,0:T(8,128)(2,1)}) custom-call(bf16[2048,768]{1,0:T(8,128)(2,1)} %bitcast.86, bf16[2048,768]{1,0:T(8,128)(2,1)} %bitcast.82, bf16[2048,768]{1,0:T(8,128)(2,1)} %bitcast.83, ...), custom_call_target="tpu_custom_call" | custom-call | flops 47185920 | bytes 25165824 | tf_op jit(solution)/shard_map/adam/pallas_call | solution.py:57
  769.3 1.4 reduce
  770.7 0.6 reshape.83
  771.3 1.4 reduce.1
  772.7 0.6 reshape.84
  (33 shorter events, 0.3 us)
Async XLA Ops:
  84.5 113.7 %copy-start.6 = (s32[16]{0:T(128)S(1)}, s32[16]{0:T(128)}, u32[]{:S(2)}) copy-start(s32[16]{0:T(128)} %param.18) | copy-start | bytes 196
  84.5 113.7 %copy-start.7 = (s32[16]{0:T(128)S(1)}, s32[16]{0:T(128)}, u32[]{:S(2)}) copy-start(s32[16]{0:T(128)} %param.19) | copy-start | bytes 196
  84.5 108.4 %all-to-all-start.2 = ((bf16[16,128,768]{2,1,0:T(8,128)(2,1)}), bf16[16,128,768]{2,1,0:T(8,128)(2,1)S(1)}, u32[]{:S(2)}, u32[]{:S(2)}) async-start(bf16[16,128,768]{2,1,0:T(8,128)(2,1)} %bitcast.88), calls=%async_computation.3 | async-start | bytes 6291456 | tf_op jit(solution)/shard_map/all_to_all | solution.py:100
  89.8 340.6 %all-gather.11.cloned.1.call-start = ((), (), s32[]{:S(2)}) async-start(), calls=%async_computation.9 | async-start | bytes 8912896 | tf_op jit(solution)/shard_map/all_gather | solution.py:111
  193.0 119.2 %all-to-all-start.4 = ((bf16[16,128,768]{2,1,0:T(8,128)(2,1)}), bf16[16,128,768]{2,1,0:T(8,128)(2,1)}, u32[]{:S(2)}, u32[]{:S(2)}) async-start(bf16[16,128,768]{2,1,0:T(8,128)(2,1)} %bitcast.89), calls=%async_computation.5 | async-start | bytes 6291456 | tf_op jit(solution)/shard_map/all_to_all | solution.py:100
  198.2 232.2 %all-gather.9.cloned.1.call-start = ((), (), s32[]{:S(2)}) async-start(), calls=%async_computation.8 | async-start | bytes 9437184 | tf_op jit(solution)/shard_map/all_gather | solution.py:124
  321.8 78.5 %copy-start.4 = (f32[128,8]{0,1:T(8,128)S(1)}, f32[128,8]{0,1:T(8,128)}, u32[]{:S(2)}) copy-start(f32[128,8]{0,1:T(8,128)} %param.16) | copy-start | bytes 12292
  321.9 78.5 %copy-start.5 = (s32[128,8]{0,1:T(8,128)S(1)}, s32[128,8]{0,1:T(8,128)}, u32[]{:S(2)}) copy-start(s32[128,8]{0,1:T(8,128)} %param.15) | copy-start | bytes 12292
  397.0 131.4 %all-gather.7.cloned.1.call-start = ((), (), s32[]{:S(2)}) async-start(), calls=%async_computation.7 | async-start | bytes 8912896 | tf_op jit(solution)/shard_map/all_gather | solution.py:112
  397.7 355.6 %reduce-scatter.2.cloned.1.call-start = ((), (), s32[]{:S(2)}) async-start(), calls=%async_computation.10 | async-start | bytes 9437184 | tf_op jit(solution)/shard_map/reduce_scatter | solution.py:132
  563.3 12.0 %copy-start.1 = (bf16[1,2048,768]{2,1,0:T(8,128)(2,1)S(1)}, bf16[1,2048,768]{2,1,0:T(8,128)(2,1)}, u32[]{:S(2)}) copy-start(bf16[1,2048,768]{2,1,0:T(8,128)(2,1)} %fusion.15) | copy-start | bytes 9437188
  578.5 81.6 %copy-start.2 = (bf16[2,1,1024]{2,0,1:T(2,128)(2,1)S(1)}, bf16[2,1,1024]{2,0,1:T(2,128)(2,1)}, u32[]{:S(2)}) copy-start(bf16[2,1,1024]{2,0,1:T(2,128)(2,1)} %param.23) | copy-start | bytes 12292
  578.5 81.6 %copy-start.3 = (bf16[2,1,1024]{2,0,1:T(2,128)(2,1)S(1)}, bf16[2,1,1024]{2,0,1:T(2,128)(2,1)}, u32[]{:S(2)}) copy-start(bf16[2,1,1024]{2,0,1:T(2,128)(2,1)} %param.24) | copy-start | bytes 12292
  653.7 99.7 %all-to-all-start.5 = ((bf16[16,128,768]{2,1,0:T(8,128)(2,1)}), bf16[16,128,768]{2,1,0:T(8,128)(2,1)S(1)}, u32[]{:S(2)}, u32[]{:S(2)}) async-start(bf16[16,128,768]{2,1,0:T(8,128)(2,1)} %get-tuple-element.40), calls=%async_computation.6 | async-start | bytes 6291456 | tf_op jit(solution)/shard_map/all_to_all | solution.py:104
  753.4 1.6 copy-start
Sparse Core Ops, SparseCore 0:
  93.4 204.4 all-gather.10
  397.1 16.0 all-gather.8
  416.0 112.3 all-gather.6
  578.6 14.2 reduce-scatter.1

commit v2 on v1

--- a/solution.py
+++ b/solution.py
@@ -24,8 +24,11 @@
     )
 
 
-def adam_kernel(grad, weight, m_code, v_code, m_scale, v_scale, noise, new_w, new_m, new_v, new_ms, new_vs):
-    grads = grad[...].astype(jnp.float32)
+def adam_kernel(parts, *refs):
+    weight, m_code, v_code, m_scale, v_scale, noise, new_w, new_m, new_v, new_ms, new_vs = refs[parts:]
+    grads = refs[0][...].astype(jnp.float32)
+    for part in refs[1:parts]:
+        grads += part[...].astype(jnp.float32)
     m_old = m_code[...].astype(jnp.float32) * (m_scale[...].astype(jnp.float32) / LEVELS)
     v_old = v_code[...].astype(jnp.float32) * (v_scale[...].astype(jnp.float32) / LEVELS)
     m_new = beta_one * m_old + (1.0 - beta_one) * grads
@@ -55,16 +58,16 @@
     big = jax.ShapeDtypeStruct((rows, width), jnp.bfloat16)
     small = jax.ShapeDtypeStruct((rows, 1), jnp.bfloat16)
     return pl.pallas_call(
-        adam_kernel,
+        functools.partial(adam_kernel, len(grads)),
         grid=(rows // block,),
         out_shape=(big, big, big, small, small),
-        in_specs=[wide, wide, wide, wide, thin, thin, wide],
+        in_specs=[wide] * len(grads) + [wide, wide, wide, thin, thin, wide],
         out_specs=(wide, wide, wide, thin, thin),
         name="adam",
         cost_estimate=pl.CostEstimate(
             flops=30 * rows * width, bytes_accessed=16 * rows * width, transcendentals=2 * rows * width
         ),
-    )(grads, weight, m_code, v_code, m_scale, v_scale, noise)
+    )(*grads, weight, m_code, v_code, m_scale, v_scale, noise)
 
 
 def on_device(
@@ -95,51 +98,73 @@
     token_count = tokens.shape[0]
     piece = 2 * rows_dp // expert_count
 
+    dp_count = lax.axis_size("dp")
+    my_dp = lax.axis_index("dp")
+
     def spread(array):
         shaped = array.reshape(expert_count, piece, hidden_units)
         return lax.all_to_all(shaped, "expert", split_axis=0, concat_axis=0, tiled=True)
 
     def collect(array):
-        regrouped = jnp.take(array, source_slot, axis=0)
-        return lax.all_to_all(regrouped, "expert", split_axis=0, concat_axis=0, tiled=True)
+        return lax.all_to_all(array, "expert", split_axis=0, concat_axis=0, tiled=True)
+
+    def regroup(array):
+        return array.at[source_slot].get(mode="promise_in_bounds")
+
+    def shift(array, step):
+        ring = [(i, (i + step) % dp_count) for i in range(dp_count)]
+        return lax.ppermute(array, "dp", ring)
 
     dense_gates = jnp.sum(
         jnp.where(routes[:, :, None] == slot_ids[None, None, :], gates[:, :, None], 0.0), axis=1
     ).T
-    all_gates = lax.all_gather(dense_gates, "expert", axis=0, tiled=False)
-    gate = lax.dynamic_index_in_dim(all_gates, my_expert, axis=1, keepdims=False).reshape(-1)
+    scales = jnp.concatenate([m_scales.reshape(-1), v_scales.reshape(-1)]).astype(jnp.float32)
+    small = jnp.concatenate([dense_gates, scales.reshape(-1, token_count)])
+    all_small = lax.all_gather(small, "expert", axis=0, tiled=False)
     all_tokens = lax.all_gather(tokens, "expert", axis=0, tiled=True)
     all_cotangent = lax.all_gather(cotangent, "expert", axis=0, tiled=True)
-    scales = jnp.concatenate([m_scales.reshape(1, 2 * rows_dp), v_scales.reshape(1, 2 * rows_dp)])
-    all_scales = lax.all_gather(scales, "expert", axis=0, tiled=False)
-    old_scales = lax.dynamic_index_in_dim(all_scales, my_source, axis=0, keepdims=False)
-
-    moved_weights = collect(spread(weights)).reshape(2, rows_dp, hidden_units)
-    moved_m = collect(spread(m_codes)).reshape(2 * rows_dp, hidden_units)
-    moved_v = collect(spread(v_codes)).reshape(2 * rows_dp, hidden_units)
-
+
+    weights, all_small = lax.optimization_barrier((weights, all_small))
+    gate = lax.dynamic_index_in_dim(all_small, my_expert, axis=1, keepdims=False).reshape(-1)
+    old_scales = lax.dynamic_index_in_dim(all_small, my_source, axis=0, keepdims=False)[expert_count:]
+    old_scales = old_scales.reshape(2, 2 * rows_dp)
+    moved_weights = collect(regroup(spread(weights)))
+    moved_weights, m_codes = lax.optimization_barrier((moved_weights, m_codes))
+    m_spread = spread(m_codes)
+    m_spread, v_codes = lax.optimization_barrier((m_spread, v_codes))
+    v_spread = spread(v_codes)
+    m_ready, v_spread = lax.optimization_barrier((regroup(m_spread), v_spread))
+    moved_m = collect(m_ready)
+    v_ready, moved_m = lax.optimization_barrier((regroup(v_spread), moved_m))
+    moved_v = collect(v_ready)
+
+    own_rows = moved_weights.reshape(2, rows_dp, hidden_units)
+    full_weights = jnp.zeros((2, dp_count * rows_dp, hidden_units), jnp.bfloat16)
+    full_weights = lax.dynamic_update_slice(full_weights, own_rows, (0, my_dp * rows_dp, 0))
+    for step in range(1, dp_count):
+        start = (my_dp - step) % dp_count * rows_dp
+        full_weights = lax.dynamic_update_slice(full_weights, shift(own_rows, step), (0, start, 0))
     gated = (gate[:, None] * all_cotangent.astype(jnp.float32)).astype(jnp.bfloat16)
     scale_model = model_width ** (-0.5)
     scale_hidden = hidden_units ** (-0.5)
-    full_weights = lax.all_gather(moved_weights, "dp", axis=1, tiled=True)
     pre = jnp.dot(all_tokens, full_weights[0], preferred_element_type=jnp.float32) * scale_model
     back = jnp.dot(gated, full_weights[1], preferred_element_type=jnp.float32) * scale_hidden
     sigmoid_pre = jax.nn.sigmoid(pre)
     hidden = (pre * sigmoid_pre).astype(jnp.bfloat16)
     pre_grad = (back * sigmoid_pre * (1.0 + pre * (1.0 - sigmoid_pre))).astype(jnp.bfloat16)
-    up_part = transposed_dot(all_tokens, pre_grad) * scale_model
-    down_part = transposed_dot(gated, hidden) * scale_hidden
-    summed = lax.psum_scatter(
-        jnp.stack([up_part.astype(jnp.bfloat16), down_part.astype(jnp.bfloat16)]),
-        "dp",
-        scatter_dimension=1,
-        tiled=True,
-    )
+    up_part = (transposed_dot(all_tokens, pre_grad) * scale_model).astype(jnp.bfloat16)
+    down_part = (transposed_dot(gated, hidden) * scale_hidden).astype(jnp.bfloat16)
+    part = jnp.stack([up_part, down_part])
+    grads = []
+    for step in range(dp_count):
+        start = (my_dp + step) % dp_count * rows_dp
+        mine = lax.dynamic_slice(part, (0, start, 0), (2, rows_dp, hidden_units))
+        grads.append((shift(mine, step) if step else mine).reshape(2 * rows_dp, hidden_units))
     new_w, new_m, new_v, new_ms, new_vs = adam(
-        summed.reshape(2 * rows_dp, hidden_units),
+        grads,
         moved_weights.reshape(2 * rows_dp, hidden_units),
-        moved_m,
-        moved_v,
+        moved_m.reshape(2 * rows_dp, hidden_units),
+        moved_v.reshape(2 * rows_dp, hidden_units),
         old_scales[0][:, None],
         old_scales[1][:, None],
         noise.reshape(2 * rows_dp, hidden_units),

time: 782 us -> 664 us (0.85)
  blocking collectives: 348 us -> 154 us
  waiting for transfers between devices: 297 us -> 349 us
  starting transfers between devices: 15.7 us -> 35 us
  local copies, waits for them, and re-layouts: 16.1 us -> 26.7 us
    all_to_all x1 -> x3, waiting for transfers between devices: 0.01 us -> 162 us  [collect(): lax.all_to_all(array, 'expert', split_axis=0, concat_axis=0, tiled=True)]
    all_to_all x2 -> x0, blocking collectives: 150 us -> none  [collect(): lax.all_to_all(regrouped, 'expert', split_axis=0, concat_axis=0, tiled=True)]
    all_gather x1, waiting for transfers between devices: 86.3 us -> 0.01 us  [on_device(): all_cotangent = lax.all_gather(cotangent, 'expert', axis=0, tiled=True)]
    all_gather x2 -> x1, blocking collectives: 120 us -> 34.4 us  [on_device(): all_small = lax.all_gather(small, 'expert', axis=0, tiled=False)]
    all_to_all x1, blocking collectives: 77.4 us -> 119 us  [spread(): lax.all_to_all(shaped, 'expert', split_axis=0, concat_axis=0, tiled=True)]
    all_to_all x2, waiting for transfers between devices: 210 us -> 185 us  [spread(): lax.all_to_all(shaped, 'expert', split_axis=0, concat_axis=0, tiled=True)]
    all_to_all x2, starting transfers between devices: 10.4 us -> 20.2 us  [spread(): lax.all_to_all(shaped, 'expert', split_axis=0, concat_axis=0, tiled=True)]
    all_to_all x1 -> x3, starting transfers between devices: 5.11 us -> 14.6 us  [collect(): lax.all_to_all(array, 'expert', split_axis=0, concat_axis=0, tiled=True)]
  transfers between devices with their start and end apart: 7 -> 9, of which waited for: 3 -> 6; matrix products, arithmetic and copies ran while one was open for 4% -> 13% of each run, Pallas kernels for 0% -> 0%
where the time goes in v2:
time: 664 us; the launch traced here: 663 us
  waiting for transfers between devices  349 us (53%)
  blocking collectives  154 us (23%)
  matrix products  58.7 us (9%)
  starting transfers between devices  35 us (5%)
  local copies, waits for them, and re-layouts  26.7 us (4%)
  between operations  18.1 us (3%)
  Pallas kernels  15.2 us (2%)
  other arithmetic  7.2 us (1%)
    all_to_all x2, waiting for transfers between devices, spread(): lax.all_to_all(shaped, 'expert', split_axis=0, concat_axis=0, tiled=True)  185 us
    all_to_all x3, waiting for transfers between devices, collect(): lax.all_to_all(array, 'expert', split_axis=0, concat_axis=0, tiled=True)  162 us
    all_to_all x1, blocking collectives, spread(): lax.all_to_all(shaped, 'expert', split_axis=0, concat_axis=0, tiled=True)  119 us
    dot_general x2, matrix products, transposed_dot(): lax.dot_general(left, right, (((0,), (0,)), ((), ())), preferred_element_...  47 us
    all_gather x1, blocking collectives, on_device(): all_small = lax.all_gather(small, 'expert', axis=0, tiled=False)  34.4 us
    all_to_all x2, starting transfers between devices, spread(): lax.all_to_all(shaped, 'expert', split_axis=0, concat_axis=0, tiled=True)  20.2 us
    pallas_call x1, Pallas kernels, adam(): pl.pallas_call(functools.partial(adam_kernel, len(grads)), grid=(rows //...  15.2 us
    all_to_all x3, starting transfers between devices, collect(): lax.all_to_all(array, 'expert', split_axis=0, concat_axis=0, tiled=True)  14.6 us
  transfers between devices with their start and end apart: 9, of which 6 were waited for; matrix products, arithmetic and copies ran while one was open for 13% of the time, Pallas kernels for 0%

profile of v2, /device:TPU:12, one launch (start us, length us, event | category | flops | bytes accessed | tf_op | source)
XLA Modules:
  0.0 663.2 jit_solution(2006267610373853872)
XLA Ops:
  7.9 0.7 concatenate.12
  8.6 0.7 concatenate.11
  9.3 0.7 select_reduce_fusion
  10.1 34.4 %all-gather = f32[768,128]{1,0:T(8,128)S(1)} all-gather(f32[48,128]{1,0:T(8,128)S(1)} %pad_maximum_fusion), channel_id=2, replica_groups=mesh['expert'=16,'dp'=2] {'expert'}, dimensions={0}, use_global_device_ids=true | all-gather | bytes 417792 | tf_op jit(solution)/shard_map/all_gather | solution.py:123
  44.4 15.2 %all-to-all-start = ((bf16[16,128,768]{2,1,0:T(8,128)(2,1)}), bf16[16,128,768]{2,1,0:T(8,128)(2,1)S(1)}, u32[]{:S(2)}, u32[]{:S(2)}) async-start(bf16[16,128,768]{2,1,0:T(8,128)(2,1)} %bitcast.88), calls=%async_computation | async-start | bytes 6291456 | tf_op jit(solution)/shard_map/all_to_all | solution.py:106
  59.8 121.0 %all-to-all-done = bf16[16,128,768]{2,1,0:T(8,128)(2,1)S(1)} async-done(((bf16[16,128,768]{2,1,0:T(8,128)(2,1)}), bf16[16,128,768]{2,1,0:T(8,128)(2,1)S(1)}, u32[]{:S(2)}, u32[]{:S(2)}) %all-to-all-start) | async-done | bytes 3145760 | tf_op jit(solution)/shard_map/all_to_all | solution.py:106
  180.8 2.4 gather_fusion
  183.2 4.4 all-to-all-start.1
  188.3 102.2 %all-to-all-done.1 = bf16[16,128,768]{2,1,0:T(8,128)(2,1)S(1)} async-done(((bf16[16,128,768]{2,1,0:T(8,128)(2,1)}), bf16[16,128,768]{2,1,0:T(8,128)(2,1)S(1)}, u32[]{:S(2)}, u32[]{:S(2)}) %all-to-all-start.1) | async-done | bytes 3145760 | tf_op jit(solution)/shard_map/all_to_all | solution.py:109
  290.5 119.1 %all_to_all.30 = bf16[16,128,768]{2,1,0:T(8,128)(2,1)} all-to-all(bf16[16,128,768]{2,1,0:T(8,128)(2,1)} %bitcast.89), channel_id=1, replica_groups=mesh['expert'=16,'dp'=2] {'expert'}, dimensions={0} | all-to-all | bytes 6291456 | tf_op jit(solution)/shard_map/all_to_all | solution.py:106
  409.7 5.0 all-to-all-start.3
  417.4 4.3 gather_fusion.1
  421.7 63.6 %all-to-all-done.3 = bf16[16,128,768]{2,1,0:T(8,128)(2,1)} async-done(((bf16[16,128,768]{2,1,0:T(8,128)(2,1)}), bf16[16,128,768]{2,1,0:T(8,128)(2,1)}, u32[]{:S(2)}, u32[]{:S(2)}) %all-to-all-start.3) | async-done | bytes 3145760 | tf_op jit(solution)/shard_map/all_to_all | solution.py:106
  485.3 5.5 all-to-all-start.4
  490.7 3.0 broadcast_in_dim.16
  493.8 1.9 constant_dynamic-update-slice_fusion.1
  495.7 3.7 constant_dynamic-update-slice_fusion
  499.4 11.7 %fusion.11 = f32[768,2048]{0,1:T(8,128)} fusion(bf16[2048,2048]{1,0:T(8,128)(2,1)} %all-gather.6.cloned.1.call-done, bf16[2,2048,768]{2,1,0:T(8,128)(2,1)} %constant_dynamic-update-slice_fusion), kind=kOutput, calls=%fused_computation.24 | convolution fusion | flops 6442450944 | bytes 17825792 | tf_op jit(solution)/shard_map/dot_general | solution.py:150
  511.1 35.0 %fusion.17 = bf16[1,2048,768]{2,1,0:T(8,128)(2,1)} fusion(bf16[2048,2048]{1,0:T(8,128)(2,1)} %all-gather.6.cloned.1.call-done, f32[768,2048]{0,1:T(8,128)} %fusion.11, bf16[2048,2048]{1,0:T(8,128)(2,1)} %all-gather.4.cloned.1.call-done, f32[2048]{0:T(1024)S(1)} %bitcast.96, bf16[2,2048,768]{2,1,0:T(8,128)(2,1)} %constant_dynamic-update-slice_fusion), kind=kOutput, calls=%fused_computation.31 | convolution fusion | flops 12917932032 | bytes 29368320 | tf_op jit(solution)/shard_map/dot_general | solution.py:22
  546.1 4.3 gather_fusion.2
  550.4 10.3 %all-to-all-done.4 = bf16[16,128,768]{2,1,0:T(8,128)(2,1)} async-done(((bf16[16,128,768]{2,1,0:T(8,128)(2,1)}), bf16[16,128,768]{2,1,0:T(8,128)(2,1)}, u32[]{:S(2)}, u32[]{:S(2)}) %all-to-all-start.4) | async-done | bytes 3145760 | tf_op jit(solution)/shard_map/all_to_all | solution.py:109
  560.8 4.8 all-to-all-start.5
  565.6 12.0 %fusion.18 = bf16[1,2048,768]{2,1,0:T(8,128)(2,1)S(1)} fusion(f32[768,2048]{0,1:T(8,128)} %fusion.11, bf16[2048,2048]{1,0:T(8,128)(2,1)} %all-gather.4.cloned.1.call-done, f32[2048]{0:T(1024)S(1)} %bitcast.97), kind=kOutput, calls=%fused_computation.32 | convolution fusion | flops 6467616768 | bytes 17833984 | tf_op jit(solution)/shard_map/dot_general | solution.py:22
  577.6 2.9 fusion.9
  582.5 1.3 copy.37.refs_5_
  583.8 1.4 copy.38.refs_6_
  585.2 1.3 collective-permute-done.1
  586.5 49.0 %all-to-all-done.5 = bf16[16,128,768]{2,1,0:T(8,128)(2,1)S(1)} async-done(((bf16[16,128,768]{2,1,0:T(8,128)(2,1)}), bf16[16,128,768]{2,1,0:T(8,128)(2,1)S(1)}, u32[]{:S(2)}, u32[]{:S(2)}) %all-to-all-start.5) | async-done | bytes 3145760 | tf_op jit(solution)/shard_map/all_to_all | solution.py:109
  635.5 1.7 copy-done.1
  637.2 15.2 %adam.1 = (bf16[2048,768]{1,0:T(8,128)(2,1)}, bf16[2048,768]{1,0:T(8,128)(2,1)}, bf16[2048,768]{1,0:T(8,128)(2,1)}, bf16[2048,1]{1,0:T(8,128)(2,1)}, bf16[2048,1]{1,0:T(8,128)(2,1)}) custom-call(bf16[2048,768]{1,0:T(8,128)(2,1)} %bitcast.86, bf16[2048,768]{1,0:T(8,128)(2,1)} %bitcast.14.refs_1_, bf16[2048,768]{1,0:T(8,128)(2,1)} %bitcast.84, ...), custom_call_target="tpu_custom_call" | custom-call | flops 47185920 | bytes 25165824 | tf_op jit(solution)/shard_map/adam/pallas_call | solution.py:60
  652.4 1.4 reduce
  654.4 1.4 reduce.1
  (28 shorter events, 3.5 us)
Async XLA Ops:
  7.2 52.5 %copy-start.3 = (s32[16]{0:T(128)S(1)}, s32[16]{0:T(128)}, u32[]{:S(2)}) copy-start(s32[16]{0:T(128)} %param.16) | copy-start | bytes 196
  7.2 52.4 %copy-start.4 = (s32[16]{0:T(128)S(1)}, s32[16]{0:T(128)}, u32[]{:S(2)}) copy-start(s32[16]{0:T(128)} %param.17) | copy-start | bytes 196
  7.2 492.2 %all-gather.6.cloned.1.call-start = ((), (), s32[]{:S(2)}) async-start(), calls=%async_computation.7 | async-start | bytes 8912896 | tf_op jit(solution)/shard_map/all_gather | solution.py:124
  44.4 136.4 %all-to-all-start = ((bf16[16,128,768]{2,1,0:T(8,128)(2,1)}), bf16[16,128,768]{2,1,0:T(8,128)(2,1)S(1)}, u32[]{:S(2)}, u32[]{:S(2)}) async-start(bf16[16,128,768]{2,1,0:T(8,128)(2,1)} %bitcast.88), calls=%async_computation | async-start | bytes 6291456 | tf_op jit(solution)/shard_map/all_to_all | solution.py:106
  183.2 107.3 %all-to-all-start.1 = ((bf16[16,128,768]{2,1,0:T(8,128)(2,1)}), bf16[16,128,768]{2,1,0:T(8,128)(2,1)S(1)}, u32[]{:S(2)}, u32[]{:S(2)}) async-start(bf16[16,128,768]{2,1,0:T(8,128)(2,1)} %gather_fusion), calls=%async_computation.1 | async-start | bytes 6291456 | tf_op jit(solution)/shard_map/all_to_all | solution.py:109
  187.6 323.5 %all-gather.4.cloned.1.call-start = ((), (), s32[]{:S(2)}) async-start(), calls=%async_computation.6 | async-start | bytes 8912896 | tf_op jit(solution)/shard_map/all_gather | solution.py:125
  290.5 203.3 %copy-start = (bf16[16,128,768]{2,1,0:T(8,128)(2,1)}, bf16[16,128,768]{2,1,0:T(8,128)(2,1)S(1)}, u32[]{:S(2)}) copy-start(bf16[16,128,768]{2,1,0:T(8,128)(2,1)S(1)} %all-to-all-done.1) | copy-start | bytes 9437188
  409.7 75.6 %all-to-all-start.3 = ((bf16[16,128,768]{2,1,0:T(8,128)(2,1)}), bf16[16,128,768]{2,1,0:T(8,128)(2,1)}, u32[]{:S(2)}, u32[]{:S(2)}) async-start(bf16[16,128,768]{2,1,0:T(8,128)(2,1)} %bitcast.90), calls=%async_computation.3 | async-start | bytes 6291456 | tf_op jit(solution)/shard_map/all_to_all | solution.py:106
  414.7 81.0 %collective-permute-start = (bf16[2,1024,768]{2,1,0:T(8,128)(2,1)S(1)}, bf16[2,1024,768]{2,1,0:T(8,128)(2,1)}, u32[]{:S(2)}, u32[]{:S(2)}) collective-permute-start(bf16[2,1024,768]{2,1,0:T(8,128)(2,1)S(1)} %bitcast.82), channel_id=1, source_target_pairs={{0,1},{1,0},{2,3},{3,2},{4,5},{5,4},{6,7},{7,6},{8,9},{9,8},{10,11... | collective-permute-start | bytes 9437192 | tf_op jit(solution)/shard_map/ppermute | solution.py:116
  485.3 75.5 %all-to-all-start.4 = ((bf16[16,128,768]{2,1,0:T(8,128)(2,1)}), bf16[16,128,768]{2,1,0:T(8,128)(2,1)}, u32[]{:S(2)}, u32[]{:S(2)}) async-start(bf16[16,128,768]{2,1,0:T(8,128)(2,1)} %gather_fusion.1), calls=%async_computation.4 | async-start | bytes 6291456 | tf_op jit(solution)/shard_map/all_to_all | solution.py:109
  560.8 74.7 %all-to-all-start.5 = ((bf16[16,128,768]{2,1,0:T(8,128)(2,1)}), bf16[16,128,768]{2,1,0:T(8,128)(2,1)S(1)}, u32[]{:S(2)}, u32[]{:S(2)}) async-start(bf16[16,128,768]{2,1,0:T(8,128)(2,1)} %gather_fusion.2), calls=%async_computation.5 | async-start | bytes 6291456 | tf_op jit(solution)/shard_map/all_to_all | solution.py:109
  565.6 12.0 %copy-start.2 = (bf16[1,2048,768]{2,1,0:T(8,128)(2,1)S(1)}, bf16[1,2048,768]{2,1,0:T(8,128)(2,1)}, u32[]{:S(2)}) copy-start(bf16[1,2048,768]{2,1,0:T(8,128)(2,1)} %fusion.17) | copy-start | bytes 9437188
  580.5 6.0 collective-permute-start.1
  635.5 1.7 copy-start.1
Sparse Core Ops, SparseCore 0:
  10.8 165.2 all-gather.5
  191.1 204.2 all-gather.3

commit v3 on v2

--- a/solution.py
+++ b/solution.py
@@ -121,14 +121,26 @@
     scales = jnp.concatenate([m_scales.reshape(-1), v_scales.reshape(-1)]).astype(jnp.float32)
     small = jnp.concatenate([dense_gates, scales.reshape(-1, token_count)])
     all_small = lax.all_gather(small, "expert", axis=0, tiled=False)
-    all_tokens = lax.all_gather(tokens, "expert", axis=0, tiled=True)
-    all_cotangent = lax.all_gather(cotangent, "expert", axis=0, tiled=True)
-
-    weights, all_small = lax.optimization_barrier((weights, all_small))
-    gate = lax.dynamic_index_in_dim(all_small, my_expert, axis=1, keepdims=False).reshape(-1)
+    inner = 1
+    while inner * inner * 4 <= expert_count and expert_count % (inner * 2) == 0:
+        inner *= 2
+    outer = expert_count // inner
+    lines = [[i + inner * k for k in range(outer)] for i in range(inner)]
+    planes = [[inner * k + i for i in range(inner)] for k in range(outer)]
+
+    def gather_rows(array):
+        line = lax.all_gather(array, "expert", axis=0, tiled=True, axis_index_groups=lines)
+        return lax.all_gather(line, "expert", axis=0, tiled=True, axis_index_groups=planes)
+
+    all_tokens = gather_rows(tokens)
+    all_cotangent = gather_rows(cotangent)
+
+    weights_ready, all_small = lax.optimization_barrier((regroup(spread(weights)), all_small))
+    gate = lax.dynamic_index_in_dim(all_small, my_expert, axis=1, keepdims=False)
+    gate = gate.reshape(outer, inner, token_count).swapaxes(0, 1).reshape(-1)
     old_scales = lax.dynamic_index_in_dim(all_small, my_source, axis=0, keepdims=False)[expert_count:]
     old_scales = old_scales.reshape(2, 2 * rows_dp)
-    moved_weights = collect(regroup(spread(weights)))
+    moved_weights = collect(weights_ready)
     moved_weights, m_codes = lax.optimization_barrier((moved_weights, m_codes))
     m_spread = spread(m_codes)
     m_spread, v_codes = lax.optimization_barrier((m_spread, v_codes))

time: 664 us -> 599 us (0.902)
  blocking collectives: 154 us -> 124 us
  waiting for transfers between devices: 349 us -> 323 us
  starting transfers between devices: 35 us -> 27.6 us
    all_gather x2 -> x4, waiting for transfers between devices: 0.01 us -> 141 us  [the longest x2 87.5 us: gather_rows(): lax.all_gather(array, 'expert', axis=0, tiled=True, axis_index_groups=lines)]
    all_to_all x3 -> x2, waiting for transfers between devices: 162 us -> 50.1 us  [collect(): lax.all_to_all(array, 'expert', split_axis=0, concat_axis=0, tiled=True)]
    all_to_all x2 -> x3, waiting for transfers between devices: 185 us -> 128 us  [spread(): lax.all_to_all(shaped, 'expert', split_axis=0, concat_axis=0, tiled=True)]
    all_to_all x1, blocking collectives: 119 us -> 68.6 us  [collect(): lax.all_to_all(array, 'expert', split_axis=0, concat_axis=0, tiled=True)]
    all_gather x1, blocking collectives: 34.4 us -> 55.3 us  [on_device(): all_small = lax.all_gather(small, 'expert', axis=0, tiled=False)]
    all_to_all x3 -> x2, starting transfers between devices: 14.6 us -> 9.36 us  [collect(): lax.all_to_all(array, 'expert', split_axis=0, concat_axis=0, tiled=True)]
    all_to_all x2 -> x3, starting transfers between devices: 20.2 us -> 18.1 us  [spread(): lax.all_to_all(shaped, 'expert', split_axis=0, concat_axis=0, tiled=True)]
  transfers between devices with their start and end apart: 9 -> 11, of which waited for: 6 -> 6; matrix products, arithmetic and copies ran while one was open for 13% -> 14% of each run, Pallas kernels for 0% -> 0%
where the time goes in v3:
time: 599 us; the launch traced here: 598 us
  waiting for transfers between devices  323 us (54%)
  blocking collectives  124 us (21%)
  matrix products  58.5 us (10%)
  starting transfers between devices  27.6 us (5%)
  local copies, waits for them, and re-layouts  25.4 us (4%)
  between operations  17.9 us (3%)
  Pallas kernels  15.2 us (3%)
  other arithmetic  6.51 us (1%)
    all_to_all x3, waiting for transfers between devices, spread(): lax.all_to_all(shaped, 'expert', split_axis=0, concat_axis=0, tiled=True)  128 us
    all_gather x2, waiting for transfers between devices, gather_rows(): lax.all_gather(array, 'expert', axis=0, tiled=True, axis_index_groups=lines)  87.5 us
    all_to_all x1, blocking collectives, collect(): lax.all_to_all(array, 'expert', split_axis=0, concat_axis=0, tiled=True)  68.6 us
    all_gather x1, blocking collectives, on_device(): all_small = lax.all_gather(small, 'expert', axis=0, tiled=False)  55.3 us
    all_gather x2, waiting for transfers between devices, gather_rows(): lax.all_gather(line, 'expert', axis=0, tiled=True, axis_index_groups=planes)  53.5 us
    all_to_all x2, waiting for transfers between devices, collect(): lax.all_to_all(array, 'expert', split_axis=0, concat_axis=0, tiled=True)  50.1 us
    dot_general x2, matrix products, transposed_dot(): lax.dot_general(left, right, (((0,), (0,)), ((), ())), preferred_element_...  46.8 us
    all_to_all x3, starting transfers between devices, spread(): lax.all_to_all(shaped, 'expert', split_axis=0, concat_axis=0, tiled=True)  18.1 us
  transfers between devices with their start and end apart: 11, of which 6 were waited for; matrix products, arithmetic and copies ran while one was open for 14% of the time, Pallas kernels for 0%

profile of v3, /device:TPU:12, one launch (start us, length us, event | category | flops | bytes accessed | tf_op | source)
XLA Modules:
  0.0 597.6 jit_solution(1788230078159350806)
XLA Ops:
  7.3 0.7 all-gather.10.cloned.1.call-update
  8.0 0.7 all-gather.6.cloned.1.call-update
  8.7 7.2 %all-to-all-start = ((bf16[16,128,768]{2,1,0:T(8,128)(2,1)}), bf16[16,128,768]{2,1,0:T(8,128)(2,1)S(1)}, u32[]{:S(2)}, u32[]{:S(2)}) async-start(bf16[16,128,768]{2,1,0:T(8,128)(2,1)} %bitcast.91), calls=%async_computation | async-start | bytes 6291456 | tf_op jit(solution)/shard_map/all_to_all | solution.py:106
  15.9 87.4 %all-gather.10.cloned.1.call-done = bf16[512,2048]{1,0:T(8,128)(2,1)} async-done(((bf16[128,2048]{1,0:T(8,128)(2,1)}), bf16[512,2048]{1,0:T(8,128)(2,1)}) %all-gather.10.cloned.1.call-update) | async-done | bytes 2097168 | tf_op jit(solution)/shard_map/all_gather | solution.py:132
  103.7 55.3 %all-gather = f32[768,128]{1,0:T(8,128)S(1)} all-gather(f32[48,128]{1,0:T(8,128)S(1)} %pad_maximum_fusion), channel_id=2, replica_groups=mesh['expert'=16,'dp'=2] {'expert'}, dimensions={0}, use_global_device_ids=true | all-gather | bytes 417792 | tf_op jit(solution)/shard_map/all_gather | solution.py:123
  159.0 2.4 gather_fusion
  161.4 68.6 %all_to_all.30 = bf16[16,128,768]{2,1,0:T(8,128)(2,1)S(1)} all-to-all(bf16[16,128,768]{2,1,0:T(8,128)(2,1)} %gather_fusion), channel_id=1, replica_groups=mesh['expert'=16,'dp'=2] {'expert'}, dimensions={0} | all-to-all | bytes 6291456 | tf_op jit(solution)/shard_map/all_to_all | solution.py:109
  230.0 5.5 all-to-all-start.2
  236.0 66.3 %all-to-all-done.2 = bf16[16,128,768]{2,1,0:T(8,128)(2,1)} async-done(((bf16[16,128,768]{2,1,0:T(8,128)(2,1)}), bf16[16,128,768]{2,1,0:T(8,128)(2,1)}, u32[]{:S(2)}, u32[]{:S(2)}) %all-to-all-start.2) | async-done | bytes 3145760 | tf_op jit(solution)/shard_map/all_to_all | solution.py:106
  302.4 5.5 all-to-all-start.3
  307.9 0.6 fusion.22
  310.5 4.3 gather_fusion.1
  314.8 62.0 %all-to-all-done.3 = bf16[16,128,768]{2,1,0:T(8,128)(2,1)} async-done(((bf16[16,128,768]{2,1,0:T(8,128)(2,1)}), bf16[16,128,768]{2,1,0:T(8,128)(2,1)}, u32[]{:S(2)}, u32[]{:S(2)}) %all-to-all-start.3) | async-done | bytes 3145760 | tf_op jit(solution)/shard_map/all_to_all | solution.py:106
  376.9 4.9 all-to-all-start.4
  381.7 3.0 broadcast_in_dim.16
  384.8 1.8 constant_dynamic-update-slice_fusion.1
  386.6 3.7 constant_dynamic-update-slice_fusion
  390.4 11.7 %fusion.11 = f32[768,2048]{0,1:T(8,128)} fusion(bf16[2048,2048]{1,0:T(8,128)(2,1)} %all-gather.12.cloned.1.call-done, bf16[2,2048,768]{2,1,0:T(8,128)(2,1)} %constant_dynamic-update-slice_fusion), kind=kOutput, calls=%fused_computation.24 | convolution fusion | flops 6442450944 | bytes 17825792 | tf_op jit(solution)/shard_map/dot_general | solution.py:162
  402.1 53.5 %all-gather.8.cloned.1.call-done = bf16[2048,2048]{1,0:T(8,128)(2,1)} async-done(((bf16[512,2048]{1,0:T(8,128)(2,1)}), bf16[2048,2048]{1,0:T(8,128)(2,1)}) %all-gather.8.cloned.1.call-update) | async-done | bytes 8388624 | tf_op jit(solution)/shard_map/all_gather | solution.py:133
  455.6 34.8 %fusion.17 = bf16[1,2048,768]{2,1,0:T(8,128)(2,1)} fusion(bf16[2048,2048]{1,0:T(8,128)(2,1)} %all-gather.12.cloned.1.call-done, f32[768,2048]{0,1:T(8,128)} %fusion.11, bf16[2048,2048]{1,0:T(8,128)(2,1)} %all-gather.8.cloned.1.call-done, f32[2048]{0:T(1024)S(1)} %bitcast.100, bf16[2,2048,768]{2,1,0:T(8,128)(2,1)} %constant_dynamic-update-slice_fusion), kind=kOutput, calls=%fused_computation.31 | convolution fusion | flops 12917932032 | bytes 29368320 | tf_op jit(solution)/shard_map/dot_general | solution.py:22
  490.4 4.3 gather_fusion.2
  494.7 4.5 all-to-all-start.5
  499.2 12.0 %fusion.18 = bf16[1,2048,768]{2,1,0:T(8,128)(2,1)S(1)} fusion(f32[768,2048]{0,1:T(8,128)} %fusion.11, bf16[2048,2048]{1,0:T(8,128)(2,1)} %all-gather.8.cloned.1.call-done, f32[2048]{0:T(1024)S(1)} %bitcast.101), kind=kOutput, calls=%fused_computation.32 | convolution fusion | flops 6467616768 | bytes 17833984 | tf_op jit(solution)/shard_map/dot_general | solution.py:22
  511.2 2.9 fusion.9
  516.1 1.4 copy.58.refs_5_
  517.5 1.3 copy.59.refs_6_
  518.8 1.3 collective-permute-done.1
  520.2 50.0 %all-to-all-done.5 = bf16[16,128,768]{2,1,0:T(8,128)(2,1)S(1)} async-done(((bf16[16,128,768]{2,1,0:T(8,128)(2,1)}), bf16[16,128,768]{2,1,0:T(8,128)(2,1)S(1)}, u32[]{:S(2)}, u32[]{:S(2)}) %all-to-all-start.5) | async-done | bytes 3145760 | tf_op jit(solution)/shard_map/all_to_all | solution.py:109
  570.2 1.7 copy-done.1
  571.9 15.2 %adam.1 = (bf16[2048,768]{1,0:T(8,128)(2,1)}, bf16[2048,768]{1,0:T(8,128)(2,1)}, bf16[2048,768]{1,0:T(8,128)(2,1)}, bf16[2048,1]{1,0:T(8,128)(2,1)}, bf16[2048,1]{1,0:T(8,128)(2,1)}) custom-call(bf16[2048,768]{1,0:T(8,128)(2,1)} %bitcast.89, bf16[2048,768]{1,0:T(8,128)(2,1)} %bitcast.16.refs_1_, bf16[2048,768]{1,0:T(8,128)(2,1)} %bitcast.87, ...), custom_call_target="tpu_custom_call" | custom-call | flops 47185920 | bytes 25165824 | tf_op jit(solution)/shard_map/adam/pallas_call | solution.py:60
  587.1 1.4 reduce
  589.1 1.4 reduce.1
  (43 shorter events, 2.2 us)
Async XLA Ops:
  7.2 96.2 %copy-start.3 = (bf16[2,1,1024]{2,0,1:T(2,128)(2,1)S(1)}, bf16[2,1,1024]{2,0,1:T(2,128)(2,1)}, u32[]{:S(2)}) copy-start(bf16[2,1,1024]{2,0,1:T(2,128)(2,1)} %param.22) | copy-start | bytes 12292
  7.2 96.2 %copy-start.4 = (bf16[2,1,1024]{2,0,1:T(2,128)(2,1)S(1)}, bf16[2,1,1024]{2,0,1:T(2,128)(2,1)}, u32[]{:S(2)}) copy-start(bf16[2,1,1024]{2,0,1:T(2,128)(2,1)} %param.21) | copy-start | bytes 12292
  7.2 96.3 %copy-start.7 = (s32[16]{0:T(128)S(1)}, s32[16]{0:T(128)}, u32[]{:S(2)}) copy-start(s32[16]{0:T(128)} %param.16) | copy-start | bytes 196
  7.2 96.3 %copy-start.8 = (s32[16]{0:T(128)S(1)}, s32[16]{0:T(128)}, u32[]{:S(2)}) copy-start(s32[16]{0:T(128)} %param.17) | copy-start | bytes 196
  7.2 96.4 %copy-start.5 = (f32[128,8]{0,1:T(8,128)S(1)}, f32[128,8]{0,1:T(8,128)}, u32[]{:S(2)}) copy-start(f32[128,8]{0,1:T(8,128)} %param.14) | copy-start | bytes 12292
  7.2 96.4 %copy-start.6 = (s32[128,8]{0,1:T(8,128)S(1)}, s32[128,8]{0,1:T(8,128)}, u32[]{:S(2)}) copy-start(s32[128,8]{0,1:T(8,128)} %param.13) | copy-start | bytes 12292
  7.2 96.1 %all-gather.10.cloned.1.call-start = ((), (), s32[]{:S(2)}) async-start(), calls=%async_computation.8 | async-start | bytes 2621440 | tf_op jit(solution)/shard_map/all_gather | solution.py:132
  8.0 227.6 %all-gather.6.cloned.1.call-start = ((), (), s32[]{:S(2)}) async-start(), calls=%async_computation.6 | async-start | bytes 2621440 | tf_op jit(solution)/shard_map/all_gather | solution.py:132
  8.7 150.3 %all-to-all-start = ((bf16[16,128,768]{2,1,0:T(8,128)(2,1)}), bf16[16,128,768]{2,1,0:T(8,128)(2,1)S(1)}, u32[]{:S(2)}, u32[]{:S(2)}) async-start(bf16[16,128,768]{2,1,0:T(8,128)(2,1)} %bitcast.91), calls=%async_computation | async-start | bytes 6291456 | tf_op jit(solution)/shard_map/all_to_all | solution.py:106
  15.9 374.5 %all-gather.12.cloned.1.call-start = ((), (), s32[]{:S(2)}) async-start(), calls=%async_computation.9 | async-start | bytes 10485760 | tf_op jit(solution)/shard_map/all_gather | solution.py:133
  230.0 154.8 %copy-start = (bf16[16,128,768]{2,1,0:T(8,128)(2,1)}, bf16[16,128,768]{2,1,0:T(8,128)(2,1)S(1)}, u32[]{:S(2)}) copy-start(bf16[16,128,768]{2,1,0:T(8,128)(2,1)S(1)} %all_to_all.30) | copy-start | bytes 9437188
  230.0 72.4 %all-to-all-start.2 = ((bf16[16,128,768]{2,1,0:T(8,128)(2,1)}), bf16[16,128,768]{2,1,0:T(8,128)(2,1)}, u32[]{:S(2)}, u32[]{:S(2)}) async-start(bf16[16,128,768]{2,1,0:T(8,128)(2,1)} %bitcast.92), calls=%async_computation.2 | async-start | bytes 6291456 | tf_op jit(solution)/shard_map/all_to_all | solution.py:106
  235.5 220.1 %all-gather.8.cloned.1.call-start = ((), (), s32[]{:S(2)}) async-start(), calls=%async_computation.7 | async-start | bytes 10485760 | tf_op jit(solution)/shard_map/all_gather | solution.py:133
  302.4 74.5 %all-to-all-start.3 = ((bf16[16,128,768]{2,1,0:T(8,128)(2,1)}), bf16[16,128,768]{2,1,0:T(8,128)(2,1)}, u32[]{:S(2)}, u32[]{:S(2)}) async-start(bf16[16,128,768]{2,1,0:T(8,128)(2,1)} %bitcast.93), calls=%async_computation.3 | async-start | bytes 6291456 | tf_op jit(solution)/shard_map/all_to_all | solution.py:106
  307.8 78.8 %collective-permute-start = (bf16[2,1024,768]{2,1,0:T(8,128)(2,1)S(1)}, bf16[2,1024,768]{2,1,0:T(8,128)(2,1)}, u32[]{:S(2)}, u32[]{:S(2)}) collective-permute-start(bf16[2,1024,768]{2,1,0:T(8,128)(2,1)S(1)} %bitcast.85), channel_id=1, source_target_pairs={{0,1},{1,0},{2,3},{3,2},{4,5},{5,4},{6,7},{7,6},{8,9},{9,8},{10,11... | collective-permute-start | bytes 9437192 | tf_op jit(solution)/shard_map/ppermute | solution.py:116
  376.9 117.9 %all-to-all-start.4 = ((bf16[16,128,768]{2,1,0:T(8,128)(2,1)}), bf16[16,128,768]{2,1,0:T(8,128)(2,1)}, u32[]{:S(2)}, u32[]{:S(2)}) async-start(bf16[16,128,768]{2,1,0:T(8,128)(2,1)} %gather_fusion.1), calls=%async_computation.4 | async-start | bytes 6291456 | tf_op jit(solution)/shard_map/all_to_all | solution.py:109
  494.7 75.5 %all-to-all-start.5 = ((bf16[16,128,768]{2,1,0:T(8,128)(2,1)}), bf16[16,128,768]{2,1,0:T(8,128)(2,1)S(1)}, u32[]{:S(2)}, u32[]{:S(2)}) async-start(bf16[16,128,768]{2,1,0:T(8,128)(2,1)} %gather_fusion.2), calls=%async_computation.5 | async-start | bytes 6291456 | tf_op jit(solution)/shard_map/all_to_all | solution.py:109
  499.2 12.0 %copy-start.2 = (bf16[1,2048,768]{2,1,0:T(8,128)(2,1)S(1)}, bf16[1,2048,768]{2,1,0:T(8,128)(2,1)}, u32[]{:S(2)}) copy-start(bf16[1,2048,768]{2,1,0:T(8,128)(2,1)} %fusion.17) | copy-start | bytes 9437188
  514.2 6.0 %collective-permute-start.1 = (bf16[2,1024,768]{2,1,0:T(8,128)(2,1)}, bf16[2,1024,768]{2,1,0:T(8,128)(2,1)}, u32[]{:S(2)}, u32[]{:S(2)}) collective-permute-start(bf16[2,1024,768]{2,1,0:T(8,128)(2,1)} %get-tuple-element.62), channel_id=1, source_target_pairs={{0,1},{1,0},{2,3},{3,2},{4,5},{5,4},{6,7},{7,6},{8,9},{9,8},{10,11... | collective-permute-start | bytes 9437192 | tf_op jit(solution)/shard_map/ppermute | solution.py:116
  570.2 1.7 copy-start.1
Sparse Core Ops, SparseCore 0:
  9.6 93.7 all-gather.9
  104.9 46.4 all-gather.5
  153.3 150.4 all-gather.11
  305.4 150.0 all-gather.7

commit v4 on v3

--- a/solution.py
+++ b/solution.py
@@ -128,12 +128,15 @@
     lines = [[i + inner * k for k in range(outer)] for i in range(inner)]
     planes = [[inner * k + i for i in range(inner)] for k in range(outer)]
 
-    def gather_rows(array):
-        line = lax.all_gather(array, "expert", axis=0, tiled=True, axis_index_groups=lines)
-        return lax.all_gather(line, "expert", axis=0, tiled=True, axis_index_groups=planes)
-
-    all_tokens = gather_rows(tokens)
-    all_cotangent = gather_rows(cotangent)
+    def gather_line(array):
+        return lax.all_gather(array, "expert", axis=0, tiled=True, axis_index_groups=lines)
+
+    def gather_plane(array):
+        return lax.all_gather(array, "expert", axis=0, tiled=True, axis_index_groups=planes)
+
+    line_tokens, all_small = lax.optimization_barrier((gather_line(tokens), all_small))
+    all_tokens = gather_plane(line_tokens)
+    all_cotangent = gather_plane(gather_line(cotangent))
 
     weights_ready, all_small = lax.optimization_barrier((regroup(spread(weights)), all_small))
     gate = lax.dynamic_index_in_dim(all_small, my_expert, axis=1, keepdims=False)
@@ -149,6 +152,7 @@
     moved_m = collect(m_ready)
     v_ready, moved_m = lax.optimization_barrier((regroup(v_spread), moved_m))
     moved_v = collect(v_ready)
+    moved_m, all_cotangent = lax.optimization_barrier((moved_m, all_cotangent))
 
     own_rows = moved_weights.reshape(2, rows_dp, hidden_units)
     full_weights = jnp.zeros((2, dp_count * rows_dp, hidden_units), jnp.bfloat16)

time: 599 us -> 565 us (0.943)
  waiting for transfers between devices: 323 us -> 195 us
  blocking collectives: 124 us -> 211 us
    all_gather x4, waiting for transfers between devices: 141 us -> 4.46 us  [the longest x2 4.44 us: gather_plane(): lax.all_gather(array, 'expert', axis=0, tiled=True, axis_index_groups=pla...]
    all_gather x1, blocking collectives: 55.3 us -> 142 us  [on_device(): all_small = lax.all_gather(small, 'expert', axis=0, tiled=False)]
    all_to_all x2, waiting for transfers between devices: 50.1 us -> 56.1 us  [collect(): lax.all_to_all(array, 'expert', split_axis=0, concat_axis=0, tiled=True)]
  transfers between devices with their start and end apart: 11 -> 11, of which waited for: 6 -> 6; matrix products, arithmetic and copies ran while one was open for 14% -> 15% of each run, Pallas kernels for 0% -> 0%
where the time goes in v4:
time: 565 us; the launch traced here: 559 us
  blocking collectives  211 us (37%)
  waiting for transfers between devices  195 us (35%)
  matrix products  59.6 us (11%)
  starting transfers between devices  27.8 us (5%)
  local copies, waits for them, and re-layouts  25.3 us (4%)
  between operations  18.4 us (3%)
  Pallas kernels  15.2 us (3%)
  other arithmetic  6.51 us (1%)
    all_gather x1, blocking collectives, on_device(): all_small = lax.all_gather(small, 'expert', axis=0, tiled=False)  142 us
    all_to_all x3, waiting for transfers between devices, spread(): lax.all_to_all(shaped, 'expert', split_axis=0, concat_axis=0, tiled=True)  131 us
    all_to_all x1, blocking collectives, collect(): lax.all_to_all(array, 'expert', split_axis=0, concat_axis=0, tiled=True)  69.1 us
    all_to_all x2, waiting for transfers between devices, collect(): lax.all_to_all(array, 'expert', split_axis=0, concat_axis=0, tiled=True)  56.1 us
    dot_general x2, matrix products, transposed_dot(): lax.dot_general(left, right, (((0,), (0,)), ((), ())), preferred_element_...  47.9 us
    all_to_all x3, starting transfers between devices, spread(): lax.all_to_all(shaped, 'expert', split_axis=0, concat_axis=0, tiled=True)  18.1 us
    pallas_call x1, Pallas kernels, adam(): pl.pallas_call(functools.partial(adam_kernel, len(grads)), grid=(rows //...  15.2 us
    dot_general x1, matrix products, on_device(): jnp.dot(all_tokens, full_weights[0], preferred_element_type=jnp.float32)  11.7 us
  transfers between devices with their start and end apart: 11, of which 6 were waited for; matrix products, arithmetic and copies ran while one was open for 15% of the time, Pallas kernels for 0%

profile of v4, /device:TPU:12, one launch (start us, length us, event | category | flops | bytes accessed | tf_op | source)
XLA Modules:
  0.0 558.8 jit_solution(3044963899587971269)
XLA Ops:
  7.3 0.7 all-gather.6.cloned.1.call-update
  8.0 7.2 %all-to-all-start = ((bf16[16,128,768]{2,1,0:T(8,128)(2,1)}), bf16[16,128,768]{2,1,0:T(8,128)(2,1)S(1)}, u32[]{:S(2)}, u32[]{:S(2)}) async-start(bf16[16,128,768]{2,1,0:T(8,128)(2,1)} %bitcast.58), calls=%async_computation | async-start | bytes 6291456 | tf_op jit(solution)/shard_map/all_to_all | solution.py:106
  15.2 0.7 all-gather.10.cloned.1.call-update
  16.1 142.0 %all-gather = f32[768,128]{1,0:T(8,128)S(1)} all-gather(f32[48,128]{1,0:T(8,128)S(1)} %pad_maximum_fusion), channel_id=2, replica_groups=mesh['expert'=16,'dp'=2] {'expert'}, dimensions={0}, use_global_device_ids=true | all-gather | bytes 417792 | tf_op jit(solution)/shard_map/all_gather | solution.py:123
  158.3 2.4 gather_fusion
  160.7 69.1 %all_to_all.30 = bf16[16,128,768]{2,1,0:T(8,128)(2,1)S(1)} all-to-all(bf16[16,128,768]{2,1,0:T(8,128)(2,1)} %gather_fusion), channel_id=1, replica_groups=mesh['expert'=16,'dp'=2] {'expert'}, dimensions={0} | all-to-all | bytes 6291456 | tf_op jit(solution)/shard_map/all_to_all | solution.py:109
  229.8 5.5 all-to-all-start.2
  235.9 66.3 %all-to-all-done.2 = bf16[16,128,768]{2,1,0:T(8,128)(2,1)} async-done(((bf16[16,128,768]{2,1,0:T(8,128)(2,1)}), bf16[16,128,768]{2,1,0:T(8,128)(2,1)}, u32[]{:S(2)}, u32[]{:S(2)}) %all-to-all-start.2) | async-done | bytes 3145760 | tf_op jit(solution)/shard_map/all_to_all | solution.py:106
  302.2 5.5 all-to-all-start.3
  307.7 4.3 gather_fusion.1
  312.0 64.7 %all-to-all-done.3 = bf16[16,128,768]{2,1,0:T(8,128)(2,1)} async-done(((bf16[16,128,768]{2,1,0:T(8,128)(2,1)}), bf16[16,128,768]{2,1,0:T(8,128)(2,1)}, u32[]{:S(2)}, u32[]{:S(2)}) %all-to-all-start.3) | async-done | bytes 3145760 | tf_op jit(solution)/shard_map/all_to_all | solution.py:106
  376.7 4.9 all-to-all-start.4
  381.6 0.6 fusion.11
  384.3 3.0 broadcast_in_dim.16
  387.3 1.8 constant_dynamic-update-slice_fusion.1
  389.1 3.7 constant_dynamic-update-slice_fusion
  392.9 11.7 %fusion.2 = f32[2048,768]{1,0:T(8,128)} fusion(bf16[2048,2048]{1,0:T(8,128)(2,1)} %all-gather.8.cloned.1.call-done, bf16[2,2048,768]{2,1,0:T(8,128)(2,1)} %constant_dynamic-update-slice_fusion), kind=kOutput, calls=%fused_computation.16 | convolution fusion | flops 6442450944 | bytes 17825792 | tf_op jit(solution)/shard_map/dot_general | solution.py:166
  404.6 4.3 gather_fusion.2
  408.9 42.1 %all-to-all-done.4 = bf16[16,128,768]{2,1,0:T(8,128)(2,1)} async-done(((bf16[16,128,768]{2,1,0:T(8,128)(2,1)}), bf16[16,128,768]{2,1,0:T(8,128)(2,1)}, u32[]{:S(2)}, u32[]{:S(2)}) %all-to-all-start.4) | async-done | bytes 3145760 | tf_op jit(solution)/shard_map/all_to_all | solution.py:109
  451.0 4.4 all-gather.12.cloned.1.call-done
  455.4 4.6 all-to-all-start.5
  460.0 35.7 %fusion.8 = bf16[1,2048,768]{2,1,0:T(8,128)(2,1)} fusion(bf16[2048,2048]{1,0:T(8,128)(2,1)} %all-gather.8.cloned.1.call-done, f32[2048,768]{1,0:T(8,128)} %fusion.2, bf16[2048,2048]{1,0:T(8,128)(2,1)} %all-gather.12.cloned.1.call-done, f32[2048]{0:T(1024)S(1)} %bitcast.67, bf16[2,2048,768]{2,1,0:T(8,128)(2,1)} %constant_dynamic-update-slice_fusion), kind=kOutput, calls=%fused_computation.23 | convolution fusion | flops 12917932032 | bytes 29368320 | tf_op jit(solution)/shard_map/dot_general | solution.py:22
  495.7 12.2 %fusion.9 = bf16[1,2048,768]{2,1,0:T(8,128)(2,1)S(1)} fusion(f32[2048,768]{1,0:T(8,128)} %fusion.2, bf16[2048,2048]{1,0:T(8,128)(2,1)} %all-gather.12.cloned.1.call-done, f32[2048]{0:T(1024)S(1)} %bitcast.68), kind=kOutput, calls=%fused_computation.24 | convolution fusion | flops 6467616768 | bytes 17833984 | tf_op jit(solution)/shard_map/dot_general | solution.py:22
  507.9 2.9 fusion
  512.9 1.4 copy.46.refs_5_
  514.2 1.3 copy.47.refs_6_
  515.6 1.3 collective-permute-done.1
  516.9 14.0 %all-to-all-done.5 = bf16[16,128,768]{2,1,0:T(8,128)(2,1)S(1)} async-done(((bf16[16,128,768]{2,1,0:T(8,128)(2,1)}), bf16[16,128,768]{2,1,0:T(8,128)(2,1)S(1)}, u32[]{:S(2)}, u32[]{:S(2)}) %all-to-all-start.5) | async-done | bytes 3145760 | tf_op jit(solution)/shard_map/all_to_all | solution.py:109
  530.9 1.7 copy-done.1
  532.6 15.2 %adam.1 = (bf16[2048,768]{1,0:T(8,128)(2,1)}, bf16[2048,768]{1,0:T(8,128)(2,1)}, bf16[2048,768]{1,0:T(8,128)(2,1)}, bf16[2048,1]{1,0:T(8,128)(2,1)}, bf16[2048,1]{1,0:T(8,128)(2,1)}) custom-call(bf16[2048,768]{1,0:T(8,128)(2,1)} %bitcast.56, bf16[2048,768]{1,0:T(8,128)(2,1)} %bitcast.16.refs_1_, bf16[2048,768]{1,0:T(8,128)(2,1)} %bitcast.54, ...), custom_call_target="tpu_custom_call" | custom-call | flops 47185920 | bytes 25165824 | tf_op jit(solution)/shard_map/adam/pallas_call | solution.py:60
  547.8 1.4 reduce
  549.8 1.4 reduce.1
  (43 shorter events, 2.2 us)
Async XLA Ops:
  7.2 8.8 %copy-start.3 = (bf16[2,1,1024]{2,0,1:T(2,128)(2,1)S(1)}, bf16[2,1,1024]{2,0,1:T(2,128)(2,1)}, u32[]{:S(2)}) copy-start(bf16[2,1,1024]{2,0,1:T(2,128)(2,1)} %param.22) | copy-start | bytes 12292
  7.2 8.8 %copy-start.4 = (bf16[2,1,1024]{2,0,1:T(2,128)(2,1)S(1)}, bf16[2,1,1024]{2,0,1:T(2,128)(2,1)}, u32[]{:S(2)}) copy-start(bf16[2,1,1024]{2,0,1:T(2,128)(2,1)} %param.21) | copy-start | bytes 12292
  7.2 8.8 %copy-start.5 = (f32[128,8]{0,1:T(8,128)S(1)}, f32[128,8]{0,1:T(8,128)}, u32[]{:S(2)}) copy-start(f32[128,8]{0,1:T(8,128)} %param.14) | copy-start | bytes 12292
  7.2 8.8 %copy-start.6 = (s32[128,8]{0,1:T(8,128)S(1)}, s32[128,8]{0,1:T(8,128)}, u32[]{:S(2)}) copy-start(s32[128,8]{0,1:T(8,128)} %param.13) | copy-start | bytes 12292
  7.2 150.9 %copy-start.7 = (s32[16]{0:T(128)S(1)}, s32[16]{0:T(128)}, u32[]{:S(2)}) copy-start(s32[16]{0:T(128)} %param.16) | copy-start | bytes 196
  7.2 150.9 %copy-start.8 = (s32[16]{0:T(128)S(1)}, s32[16]{0:T(128)}, u32[]{:S(2)}) copy-start(s32[16]{0:T(128)} %param.17) | copy-start | bytes 196
  7.2 150.9 %all-gather.6.cloned.1.call-start = ((), (), s32[]{:S(2)}) async-start(), calls=%async_computation.6 | async-start | bytes 2621440 | tf_op jit(solution)/shard_map/all_gather | solution.py:132
  8.0 150.3 %all-to-all-start = ((bf16[16,128,768]{2,1,0:T(8,128)(2,1)}), bf16[16,128,768]{2,1,0:T(8,128)(2,1)S(1)}, u32[]{:S(2)}, u32[]{:S(2)}) async-start(bf16[16,128,768]{2,1,0:T(8,128)(2,1)} %bitcast.58), calls=%async_computation | async-start | bytes 6291456 | tf_op jit(solution)/shard_map/all_to_all | solution.py:106
  15.1 220.2 %all-gather.10.cloned.1.call-start = ((), (), s32[]{:S(2)}) async-start(), calls=%async_computation.8 | async-start | bytes 2621440 | tf_op jit(solution)/shard_map/all_gather | solution.py:132
  15.9 377.0 %all-gather.8.cloned.1.call-start = ((), (), s32[]{:S(2)}) async-start(), calls=%async_computation.7 | async-start | bytes 10485760 | tf_op jit(solution)/shard_map/all_gather | solution.py:135
  229.8 157.5 %copy-start = (bf16[16,128,768]{2,1,0:T(8,128)(2,1)}, bf16[16,128,768]{2,1,0:T(8,128)(2,1)S(1)}, u32[]{:S(2)}) copy-start(bf16[16,128,768]{2,1,0:T(8,128)(2,1)S(1)} %all_to_all.30) | copy-start | bytes 9437188
  229.8 72.4 %all-to-all-start.2 = ((bf16[16,128,768]{2,1,0:T(8,128)(2,1)}), bf16[16,128,768]{2,1,0:T(8,128)(2,1)}, u32[]{:S(2)}, u32[]{:S(2)}) async-start(bf16[16,128,768]{2,1,0:T(8,128)(2,1)} %bitcast.59), calls=%async_computation.2 | async-start | bytes 6291456 | tf_op jit(solution)/shard_map/all_to_all | solution.py:106
  235.3 220.1 %all-gather.12.cloned.1.call-start = ((), (), s32[]{:S(2)}) async-start(), calls=%async_computation.9 | async-start | bytes 10485760 | tf_op jit(solution)/shard_map/all_gather | solution.py:135
  302.2 74.5 %all-to-all-start.3 = ((bf16[16,128,768]{2,1,0:T(8,128)(2,1)}), bf16[16,128,768]{2,1,0:T(8,128)(2,1)}, u32[]{:S(2)}, u32[]{:S(2)}) async-start(bf16[16,128,768]{2,1,0:T(8,128)(2,1)} %bitcast.60), calls=%async_computation.3 | async-start | bytes 6291456 | tf_op jit(solution)/shard_map/all_to_all | solution.py:106
  376.7 74.3 %all-to-all-start.4 = ((bf16[16,128,768]{2,1,0:T(8,128)(2,1)}), bf16[16,128,768]{2,1,0:T(8,128)(2,1)}, u32[]{:S(2)}, u32[]{:S(2)}) async-start(bf16[16,128,768]{2,1,0:T(8,128)(2,1)} %gather_fusion.1), calls=%async_computation.4 | async-start | bytes 6291456 | tf_op jit(solution)/shard_map/all_to_all | solution.py:109
  381.6 7.6 %collective-permute-start = (bf16[2,1024,768]{2,1,0:T(8,128)(2,1)S(1)}, bf16[2,1024,768]{2,1,0:T(8,128)(2,1)}, u32[]{:S(2)}, u32[]{:S(2)}) collective-permute-start(bf16[2,1024,768]{2,1,0:T(8,128)(2,1)S(1)} %bitcast.52), channel_id=1, source_target_pairs={{0,1},{1,0},{2,3},{3,2},{4,5},{5,4},{6,7},{7,6},{8,9},{9,8},{10,11... | collective-permute-start | bytes 9437192 | tf_op jit(solution)/shard_map/ppermute | solution.py:116
  455.4 75.5 %all-to-all-start.5 = ((bf16[16,128,768]{2,1,0:T(8,128)(2,1)}), bf16[16,128,768]{2,1,0:T(8,128)(2,1)S(1)}, u32[]{:S(2)}, u32[]{:S(2)}) async-start(bf16[16,128,768]{2,1,0:T(8,128)(2,1)} %gather_fusion.2), calls=%async_computation.5 | async-start | bytes 6291456 | tf_op jit(solution)/shard_map/all_to_all | solution.py:109
  495.7 12.2 %copy-start.2 = (bf16[1,2048,768]{2,1,0:T(8,128)(2,1)S(1)}, bf16[1,2048,768]{2,1,0:T(8,128)(2,1)}, u32[]{:S(2)}) copy-start(bf16[1,2048,768]{2,1,0:T(8,128)(2,1)} %fusion.8) | copy-start | bytes 9437188
  510.9 6.0 %collective-permute-start.1 = (bf16[2,1024,768]{2,1,0:T(8,128)(2,1)}, bf16[2,1024,768]{2,1,0:T(8,128)(2,1)}, u32[]{:S(2)}, u32[]{:S(2)}) collective-permute-start(bf16[2,1024,768]{2,1,0:T(8,128)(2,1)} %get-tuple-element.70), channel_id=1, source_target_pairs={{0,1},{1,0},{2,3},{3,2},{4,5},{5,4},{6,7},{7,6},{8,9},{9,8},{10,11... | collective-permute-start | bytes 9437192 | tf_op jit(solution)/shard_map/ppermute | solution.py:116
  530.9 1.7 copy-start.1
Sparse Core Ops, SparseCore 0:
  9.6 93.3 all-gather.5
  104.6 46.4 all-gather.9
  158.2 145.1 all-gather.7
  305.1 150.2 all-gather.11
